TPU v7x, 32 devices: a whole 2x2x4 slice. The times are simulated.
32 devices in a mesh: dp: 16 (over z, x, core), depth: 2 (over y).
Axes of the slice: x: 2, y: 2, z: 4, core: 2. Of those that a mesh axis runs over, the one named last changes fastest.
Arguments:
- volume: bfloat16 [16, 4, 4, 8, 128], P('dp', None, 'depth'), may hold values from -6 to 6
- kernel_one: bfloat16 [32, 4, 3, 3, 3], replicated, may hold values from -0.625 to 0.625
- bias_one: float32 [32], replicated, may hold values from -0.5 to 0.5
- kernel_two: bfloat16 [64, 32, 3, 3, 3], replicated, may hold values from -0.21875 to 0.21875
- bias_two: float32 [64], replicated, may hold values from -0.5 to 0.5
- cotangent: bfloat16 [16, 64, 4, 8, 128], P('dp', None, 'depth'), may hold values from -0.0234375 to 0.0234375
Outputs:
- features: bfloat16 [16, 64, 4, 8, 128], P('dp', None, 'depth')
- grad_kernel_one: float32 [32, 4, 3, 3, 3], replicated
- grad_bias_one: float32 [32], replicated
- grad_kernel_two: float32 [64, 32, 3, 3, 3], replicated
- grad_bias_two: float32 [64], replicated
All inputs are finite; a program needn't handle non-finite values.
Results may differ from a plain program's by a relative error of at most 0.006.
Values may be sent and summed in bfloat16 or wider, within the bound.
A program may use at most 64 MiB of HBM per device.

v0:
```python
import jax
import jax.numpy as jnp
from jax import lax
from jax.sharding import PartitionSpec as P

FORWARD_DIMS = ("NCDHW", "OIDHW", "NCDHW")
KERNEL_DIMS = ("CNDHW", "IODHW", "CNDHW")


def extended(x, sides, width):
    for axis, dim in sides:
        size, length = (lax.axis_size(axis), x.shape[dim])
        up = [(i, (i + 1) % size) for i in range(size - 1)]
        down = [(j, i) for i, j in up]
        last = lax.slice_in_dim(x, length - width, length, axis=dim)
        leading = lax.slice_in_dim(x, 0, width, axis=dim)
        before = lax.ppermute(last, axis, up)
        after = lax.ppermute(leading, axis, down)
        x = jnp.concatenate([before, x, after], axis=dim)
    return x


def convolve(inputs, kernel, depth_pad=0):
    return lax.conv_general_dilated(
        inputs,
        kernel,
        (1, 1, 1),
        ((depth_pad, depth_pad), (1, 1), (1, 1)),
        dimension_numbers=FORWARD_DIMS,
        preferred_element_type=jnp.float32,
    )


def kernel_grad(inputs, slope):
    return lax.conv_general_dilated(
        inputs,
        slope,
        (1, 1, 1),
        ((0, 0), (1, 1), (1, 1)),
        dimension_numbers=KERNEL_DIMS,
        preferred_element_type=jnp.float32,
    )


def silu_slope(value):
    sig = jax.nn.sigmoid(value)
    return sig * (1.0 + value * (1.0 - sig))


def per_device(volume, kernel_one, bias_one, kernel_two, bias_two, cotangent):
    planes = volume.shape[2]
    shift_one = bias_one[None, :, None, None, None]
    padded = extended(volume, (("depth", 2),), 2)
    pre_wide = convolve(padded, kernel_one) + shift_one
    global_plane = lax.axis_index("depth") * planes + jnp.arange(planes + 2, dtype=jnp.int32) - 1
    inside = (global_plane >= 0) & (global_plane < planes * lax.axis_size("depth"))
    inside = inside.astype(jnp.float32)[None, None, :, None, None]
    act_wide = (jax.nn.silu(pre_wide) * inside).astype(jnp.bfloat16)
    pre_one = pre_wide[:, :, 1:-1]
    input_wide = padded[:, :, 1:-1]
    pre_two = convolve(act_wide, kernel_two) + bias_two[None, :, None, None, None]
    features = jax.nn.silu(pre_two).astype(jnp.bfloat16)
    slope_two = (cotangent.astype(jnp.float32) * silu_slope(pre_two)).astype(jnp.bfloat16)
    grad_two = kernel_grad(act_wide, slope_two)
    bias_grad_two = jnp.sum(slope_two, axis=(0, 2, 3, 4), dtype=jnp.float32)
    flipped = jnp.transpose(jnp.flip(kernel_two, (2, 3, 4)), (1, 0, 2, 3, 4))
    slope_wide = extended(slope_two, (("depth", 2),), 1)
    back_one = convolve(slope_wide, flipped)
    slope_one = (back_one * silu_slope(pre_one)).astype(jnp.bfloat16)
    grad_one = kernel_grad(input_wide, slope_one)
    bias_grad_one = jnp.sum(slope_one, axis=(0, 2, 3, 4), dtype=jnp.float32)
    grad_one, bias_grad_one, grad_two, bias_grad_two = lax.psum(
        (grad_one, bias_grad_one, grad_two, bias_grad_two), ("dp", "depth")
    )
    return (features, grad_one, bias_grad_one, grad_two, bias_grad_two)


def solution(mesh):
    return jax.shard_map(
        per_device,
        mesh=mesh,
        in_specs=(
            P("dp", None, "depth", None, None),
            P(),
            P(),
            P(),
            P(),
            P("dp", None, "depth", None, None),
        ),
        out_specs=(P("dp", None, "depth", None, None), P(), P(), P(), P()),
        check_vma=False,
    )
```

profile of v0, /device:TPU:0, one launch (start us, length us, event | category | flops | bytes accessed | tf_op | source)
XLA Modules:
  0.0 180.4 jit_solution(6209698671688462025)
XLA Ops:
  7.2 5.0 %collective-permute-start = (bf16[1,4,2,8,128]{4,3,2,1,0:T(8,128)(2,1)}, bf16[1,4,2,8,128]{4,3,2,1,0:T(8,128)(2,1)S(1)}, u32[]{:S(2)}, u32[]{:S(2)}) collective-permute-start(bf16[1,4,2,8,128]{4,3,2,1,0:T(8,128)(2,1)} %param.6), channel_id=1, source_target_pairs={{0,1},{2,3},{4,5},{6,7},{8,9},{10,11},{12,13},{14,15},{16,17},{18,... | collective-permute-start | bytes 49160 | tf_op jit(solution)/shard_map/ppermute | solution.py:17
  12.3 1.3 collective-permute-start.1
  13.6 1.4 copy.76
  15.0 3.1 %collective-permute-done.1 = bf16[1,4,2,8,128]{4,3,2,1,0:T(8,128)(2,1)S(1)} collective-permute-done((bf16[1,4,2,8,128]{4,3,2,1,0:T(8,128)(2,1)}, bf16[1,4,2,8,128]{4,3,2,1,0:T(8,128)(2,1)S(1)}, u32[]{:S(2)}, u32[]{:S(2)}) %collective-permute-start.1) | collective-permute-done | bytes 16416 | tf_op jit(solution)/shard_map/ppermute | solution.py:18
  19.3 1.4 copy.69
  20.8 6.8 %fusion.23 = (bf16[4,8,8,17,32]{4,2,3,1,0:T(8,128)(2,1)S(1)}, f32[4,8,8,17,32]{4,2,3,1,0:T(8,128)}) fusion(f32[4]{0:T(128)S(1)} %and_convert_fusion, pred[8,17]{0,1:T(8,128)(4,1)S(1)} %copy-done.12, f32[32]{0:T(128)S(1)} %copy-done.10, bf16[32,4,3,3,3]{0,1,4,3,2:T(4,128)(2,1)S(1)} %copy-done.9, bf16[4,6,8,1,7,2]{4,0,5,2,1,3:T(4,128)(2,1)S(1)} %slice.28, ...), kind=kOutput, calls=%fused_computation.37 | convolution fusion | flops 29002752 | bytes 900376 | tf_op jit(solution)/shard_map/conv_general_dilated | solution.py:24
  28.3 1.3 fusion.53
  32.1 1.1 reshape.62
  34.1 2.7 %add_multiply_fusion = (f32[2,8,8,17,64]{4,2,3,1,0:T(8,128)S(1)}, bf16[2,8,8,17,64]{4,2,3,1,0:T(8,128)(2,1)}) fusion(f32[64]{0:T(128)S(1)} %copy-done.11, bf16[64,32,3,3,3]{0,1,4,3,2:T(8,128)(2,1)S(1)} %copy-done, bf16[4,8,1,8,1,32]{5,3,4,1,0,2:T(8,128)(2,1)S(1)} %pad.3, bf16[4,8,1,8,17,32]{5,3,4,1,0,2:T(8,128)(2,1)S(1)} %bitcast.71, ...), kind=kOutput, calls=%fused_computation.34 | convolution fusion | flops 222920704 | bytes 1257728 | tf_op jit(solution)/shard_map/conv_general_dilated | solution.py:24
  39.2 4.8 %fusion.19 = f32[64,32,3,3,3]{0,1,4,3,2:T(8,128)} fusion(bf16[64,2,8,8,17,1]{0,2,4,3,1,5:T(8,128)(2,1)S(1)} %bitcast.75, bf16[4,8,8,17,32,1]{4,2,3,1,0,5:T(8,128)(2,1)S(1)} %get-tuple-element.51, bf16[4,8,8,17,32,1]{4,2,3,1,0,5:T(8,128)(2,1)S(1)} %bitcast.72, bf16[4,8,8,17,32,1]{4,2,3,1,0,5:T(8,128)(2,1)S(1)} %get-tuple-element.50), kind=kOutput, calls=%fused_computation.29 | convolution fusion | flops 221429760 | bytes 1335296 | tf_op jit(solution)/shard_map/conv_general_dilated | solution.py:35
  44.0 2.5 %collective-permute-start.2 = (bf16[1,64,1,8,128]{1,3,4,2,0:T(8,128)(2,1)}, bf16[1,64,1,8,128]{1,3,4,2,0:T(8,128)(2,1)}, u32[]{:S(2)}, u32[]{:S(2)}) collective-permute-start(bf16[1,64,1,8,128]{1,3,4,2,0:T(8,128)(2,1)} %get-tuple-element.36), channel_id=1, source_target_pairs={{0,1},{2,3},{4,5},{6,7},{8,9},{10,11},{12,13},{14,15},{16,17},{18,... | collective-permute-start | bytes 393224 | tf_op jit(solution)/shard_map/ppermute | solution.py:17
  46.5 1.3 collective-permute-start.3
  48.5 1.6 copy.86
  50.1 1.2 copy.84
  51.3 1.9 %copy.87 = bf16[4,6,8,1,7,1]{4,0,5,2,1,3:T(4,128)(2,1)} copy(bf16[4,6,8,1,7,1]{5,4,2,1,0,3:T(8,128)(2,1)S(1)} %copy-done.2) | data formatting | bytes 5376
  53.2 2.1 %copy.75 = bf16[4,6,8,8,17,1]{3,0,5,4,2,1:T(4,128)(2,1)} copy(bf16[4,6,8,8,17,1]{4,3,2,1,0,5:T(8,128)(2,1)S(1)} %copy-done.4) | data formatting | bytes 104448 | tf_op jit(solution)/shard_map/concatenate | solution.py:19
  55.4 1.1 copy.83
  57.5 1.3 maximum_bitcast_fusion.4
  59.3 1.4 copy-done.13
  60.7 4.4 %select_reduce_fusion = (f32[32]{0:T(128)S(1)}, bf16[2,8,8,17,32]{4,2,3,1,0:T(8,128)(2,1)S(1)}) fusion(pred[8,17]{0,1:T(8,128)(4,1)S(1)} %copy-done.12, f32[4,8,8,17,32]{4,2,3,1,0:T(8,128)S(1)} %copy-done.13, bf16[64,32,3,3,3]{0,1,4,3,2:T(8,128)(2,1)S(1)} %copy-done, bf16[64,4,8,1,7,2]{0,4,5,2,1,3:T(8,128)(2,1)S(1)} %slice.39, ...), kind=kOutput, calls=%fused_computation.33 | convolution fusion | flops 223367136 | bytes 1143048 | tf_op jit(solution)/shard_map/conv_general_dilated | solution.py:24
  65.0 3.8 %fusion.22 = f32[32,4,3,3,3]{0,1,4,3,2:T(4,128)S(1)} fusion(bf16[4,6,8,8,17,1]{3,0,5,4,2,1:T(4,128)(2,1)S(1)} %get-tuple-element.48, bf16[4,6,8,8,17,1]{3,0,5,4,2,1:T(4,128)(2,1)S(1)} %copy-done.6, bf16[4,6,8,8,17,1]{3,0,5,4,2,1:T(4,128)(2,1)S(1)} %get-tuple-element.49, bf16[2,8,8,17,32]{4,2,3,1,0:T(8,128)(2,1)S(1)} %get-tuple-element.47, ...), kind=kOutput, calls=%fused_computation.30 | convolution fusion | flops 14326784 | bytes 309896 | tf_op jit(solution)/shard_map/conv_general_dilated | solution.py:35
  68.8 43.4 %all-reduce = (f32[32,4,3,3,3]{0,1,4,3,2:T(4,128)}, f32[32]{0:T(128)}, f32[64]{0:T(128)}) all-reduce(f32[32,4,3,3,3]{0,1,4,3,2:T(4,128)S(1)} %fusion.22, f32[32]{0:T(128)S(1)} %get-tuple-element.46, f32[64]{0:T(128)S(1)} %get-tuple-element.28), channel_id=1, replica_groups=mesh['dp'=16,'depth'=2] {'dp','depth'}, use_global_device_ids=true, to_apply=%region_0.1 | all-reduce | flops 3552 | bytes 28416 | tf_op jit(solution)/shard_map/psum | solution.py:72
  112.3 59.5 %all-reduce.3.cloned.1.call-done = f32[64,32,3,3,3]{0,1,4,3,2:T(8,128)} async-done(((f32[64,32,3,3,3]{0,1,4,3,2:T(8,128)}), f32[64,32,3,3,3]{0,1,4,3,2:T(8,128)}) %all-reduce.3.cloned.1.call-update) | async-done | bytes 221200 | tf_op jit(solution)/shard_map/psum | solution.py:72
  171.8 1.8 copy.95
  (55 shorter events, 9.8 us)
Async XLA Ops:
  7.2 26.9 %copy-start = (bf16[64,32,3,3,3]{0,1,4,3,2:T(8,128)(2,1)S(1)}, bf16[64,32,3,3,3]{0,1,4,3,2:T(8,128)(2,1)}, u32[]{:S(2)}) copy-start(bf16[64,32,3,3,3]{0,1,4,3,2:T(8,128)(2,1)} %param.9) | copy-start | bytes 331780
  7.2 164.6 %all-reduce.3.cloned.1.call-start = ((), (), s32[]{:S(2)}) async-start(), calls=%async_computation | async-start | bytes 884736 | tf_op jit(solution)/shard_map/psum | solution.py:72
  7.2 7.8 %collective-permute-start = (bf16[1,4,2,8,128]{4,3,2,1,0:T(8,128)(2,1)}, bf16[1,4,2,8,128]{4,3,2,1,0:T(8,128)(2,1)S(1)}, u32[]{:S(2)}, u32[]{:S(2)}) collective-permute-start(bf16[1,4,2,8,128]{4,3,2,1,0:T(8,128)(2,1)} %param.6), channel_id=1, source_target_pairs={{0,1},{2,3},{4,5},{6,7},{8,9},{10,11},{12,13},{14,15},{16,17},{18,... | collective-permute-start | bytes 49160 | tf_op jit(solution)/shard_map/ppermute | solution.py:17
  12.3 5.8 %collective-permute-start.1 = (bf16[1,4,2,8,128]{4,3,2,1,0:T(8,128)(2,1)}, bf16[1,4,2,8,128]{4,3,2,1,0:T(8,128)(2,1)S(1)}, u32[]{:S(2)}, u32[]{:S(2)}) collective-permute-start(bf16[1,4,2,8,128]{4,3,2,1,0:T(8,128)(2,1)} %param.6), channel_id=1, source_target_pairs={{1,0},{3,2},{5,4},{7,6},{9,8},{11,10},{13,12},{15,14},{17,16},{19,... | collective-permute-start | bytes 49160 | tf_op jit(solution)/shard_map/ppermute | solution.py:18
  15.0 5.8 %copy-start.9 = (bf16[32,4,3,3,3]{0,1,4,3,2:T(4,128)(2,1)S(1)}, bf16[32,4,3,3,3]{0,1,4,3,2:T(4,128)(2,1)}, u32[]{:S(2)}) copy-start(bf16[32,4,3,3,3]{0,1,4,3,2:T(4,128)(2,1)} %param.7) | copy-start | bytes 20740
  15.0 5.8 %copy-start.10 = (f32[32]{0:T(128)S(1)}, f32[32]{0:T(128)}, u32[]{:S(2)}) copy-start(f32[32]{0:T(128)} %param.8) | copy-start | bytes 388
  15.0 5.8 %copy-start.12 = (pred[8,17]{0,1:T(8,128)(4,1)S(1)}, pred[8,17]{0,1:T(8,128)(4,1)}, u32[]{:S(2)}) copy-start(pred[8,17]{0,1:T(8,128)(4,1)} %constant.46) | copy-start | bytes 412
  31.0 3.1 %copy-start.11 = (f32[64]{0:T(128)S(1)}, f32[64]{0:T(128)}, u32[]{:S(2)}) copy-start(f32[64]{0:T(128)} %param.10) | copy-start | bytes 772
  37.3 1.4 copy-start.1
  39.2 8.6 %copy-start.5 = (bf16[4,6,8,1,8,16]{5,4,2,1,0,3:T(8,128)(2,1)S(1)}, bf16[4,6,8,1,8,16]{5,4,2,1,0,3:T(8,128)(2,1)}, u32[]{:S(2)}) copy-start(bf16[4,6,8,1,8,16]{5,4,2,1,0,3:T(8,128)(2,1)} %get-tuple-element.38) | copy-start | bytes 147460
  44.0 6.0 %copy-start.3 = (bf16[4,6,8,1,7,1]{5,4,2,1,0,3:T(8,128)(2,1)S(1)}, bf16[4,6,8,1,7,1]{5,4,2,1,0,3:T(8,128)(2,1)}, u32[]{:S(2)}) copy-start(bf16[4,6,8,1,7,1]{5,4,2,1,0,3:T(8,128)(2,1)} %get-tuple-element.40) | copy-start | bytes 8068
  44.0 13.5 %collective-permute-start.2 = (bf16[1,64,1,8,128]{1,3,4,2,0:T(8,128)(2,1)}, bf16[1,64,1,8,128]{1,3,4,2,0:T(8,128)(2,1)}, u32[]{:S(2)}, u32[]{:S(2)}) collective-permute-start(bf16[1,64,1,8,128]{1,3,4,2,0:T(8,128)(2,1)} %get-tuple-element.36), channel_id=1, source_target_pairs={{0,1},{2,3},{4,5},{6,7},{8,9},{10,11},{12,13},{14,15},{16,17},{18,... | collective-permute-start | bytes 393224 | tf_op jit(solution)/shard_map/ppermute | solution.py:17
  46.5 11.0 %collective-permute-start.3 = (bf16[1,64,1,8,128]{1,3,4,2,0:T(8,128)(2,1)}, bf16[1,64,1,8,128]{1,3,4,2,0:T(8,128)(2,1)}, u32[]{:S(2)}, u32[]{:S(2)}) collective-permute-start(bf16[1,64,1,8,128]{1,3,4,2,0:T(8,128)(2,1)} %get-tuple-element.37), channel_id=1, source_target_pairs={{1,0},{3,2},{5,4},{7,6},{9,8},{11,10},{13,12},{15,14},{17,16},{19,... | collective-permute-start | bytes 393224 | tf_op jit(solution)/shard_map/ppermute | solution.py:18
  47.8 3.5 %copy-start.2 = (bf16[4,6,8,1,7,1]{5,4,2,1,0,3:T(8,128)(2,1)S(1)}, bf16[4,6,8,1,7,1]{5,4,2,1,0,3:T(8,128)(2,1)}, u32[]{:S(2)}) copy-start(bf16[4,6,8,1,7,1]{5,4,2,1,0,3:T(8,128)(2,1)} %get-tuple-element.41) | copy-start | bytes 8068
  48.5 4.7 %copy-start.4 = (bf16[4,6,8,8,17,1]{4,3,2,1,0,5:T(8,128)(2,1)S(1)}, bf16[4,6,8,8,17,1]{4,3,2,1,0,5:T(8,128)(2,1)}, u32[]{:S(2)}) copy-start(bf16[4,6,8,8,17,1]{4,3,2,1,0,5:T(8,128)(2,1)} %reshape.62) | copy-start | bytes 156676
  53.2 2.1 %copy-start.7 = (bf16[2,8,8,17,64]{4,2,3,1,0:T(8,128)(2,1)S(1)}, bf16[2,8,8,17,64]{4,2,3,1,0:T(8,128)(2,1)}, u32[]{:S(2)}) copy-start(bf16[2,8,8,17,64]{4,2,3,1,0:T(8,128)(2,1)} %get-tuple-element.33) | copy-start | bytes 835588
  55.3 1.3 copy-start.8
  59.0 1.6 copy-start.13
  60.7 4.4 %copy-start.6 = (bf16[4,6,8,8,17,1]{3,0,5,4,2,1:T(4,128)(2,1)S(1)}, bf16[4,6,8,8,17,1]{3,0,5,4,2,1:T(4,128)(2,1)}, u32[]{:S(2)}) copy-start(bf16[4,6,8,8,17,1]{3,0,5,4,2,1:T(4,128)(2,1)} %copy.75) | copy-start | bytes 156676
Sparse Core Ops, SparseCore 0:
  44.1 127.5 all-reduce.2
where the time goes:
time: 181 us; the launch traced here: 180 us
  waiting for transfers between devices  62.6 us (35%)
  blocking collectives  43.4 us (24%)
  local copies, waits for them, and re-layouts  23.7 us (13%)
  matrix products  22.5 us (12%)
  between operations  14.4 us (8%)
  starting transfers between devices  10.1 us (6%)
  other arithmetic  3.68 us (2%)
    psum x1, waiting for transfers between devices, per_device(): lax.psum((grad_one, bias_grad_one, grad_two, bias_grad_two), ('dp', 'dept...  59.5 us
    psum x1, blocking collectives, per_device(): lax.psum((grad_one, bias_grad_one, grad_two, bias_grad_two), ('dp', 'dept...  43.4 us
    conv_general_dilated x3, matrix products, convolve(): lax.conv_general_dilated(inputs, kernel, (1, 1, 1), ((depth_pad, depth_pa...  13.9 us
    unnamed x35, local copies, waits for them, and re-layouts  11.6 us
    conv_general_dilated x2, matrix products, kernel_grad(): lax.conv_general_dilated(inputs, slope, (1, 1, 1), ((0, 0), (1, 1), (1, 1...  8.58 us
    ppermute x2, starting transfers between devices, extended(): before = lax.ppermute(last, axis, up)  7.52 us
    concatenate x7, local copies, waits for them, and re-layouts, extended(): x = jnp.concatenate([before, x, after], axis=dim)  5.95 us
  transfers between devices with their start and end apart: 5, of which 2 were waited for; matrix products, arithmetic and copies ran while one was open for 12% of the time, Pallas kernels for 0%

commit v1 on v0

v1 whole, which is shorter than its diff:
```python
import functools

import jax
import jax.numpy as jnp
from jax import lax
from jax.experimental import pallas as pl
from jax.experimental.pallas import tpu as pltpu
from jax.sharding import PartitionSpec as P

F32 = jnp.float32
BF16 = jnp.bfloat16
MESH = pl.DeviceIdType.MESH
ROWS = 16
NT = (((1,), (1,)), ((), ()))


def kernel(n, nd, vol, w1, b1, w2, b2, cot, feat, g1_o, gb1_o, g2_o, gb2_o,
           vrecv, v32, stack_v, cot32, d_one, stack_a, res, slope3, sl, srecv,
           stack_s, feat32, slope31, sb, rb, red, gath,
           vs_sem, vr_sem, ss_sem, sr_sem, p1s, p1r, p2s, p2r):
    cin, planes, ny, nx = vol.shape
    cone, ctwo = w2.shape[1], w2.shape[2]
    cells = planes * ny * nx
    plane = ny * nx
    wide = planes + 2
    nsh = sb.shape[0]
    stride = n // nsh
    early = (27 * cone * ctwo // nx) // ROWS

    de = lax.axis_index("depth")
    me = lax.axis_index("dp") * nd + de
    dp = lax.axis_index("dp")

    def dev(t):
        return (lax.div(t, nd), lax.rem(t, nd))

    bar = pltpu.get_barrier_semaphore()

    @pl.loop(1, n)
    def _(d):
        pl.semaphore_signal(bar, inc=1, device_id=dev(lax.rem(me + d, n)), device_id_type=MESH)

    cot32[...] = cot[...].astype(F32).reshape(cot32.shape)
    wz = planes + 4
    zero8 = jnp.zeros((ny, nx), F32)
    for ch in range(8):
        for z in range(planes if ch < cin else wz):
            if ch < cin:
                v32[pl.ds((ch * wz + z + 2) * ny, ny), :] = vol[ch, z].astype(F32)
            else:
                v32[pl.ds((ch * wz + z) * ny, ny), :] = zero8
    lhs1 = []
    for ab in range(9):
        row = jnp.concatenate([w1[ab * 3 + c].astype(F32) for c in range(3)], axis=1)
        lhs1.append(jnp.concatenate([row, jnp.zeros((8 - cin, 3 * cone), F32)], axis=0))
    lhs1 = jnp.transpose(jnp.concatenate(lhs1, axis=0)).astype(BF16)
    lhs2 = jnp.concatenate(
        [jnp.concatenate([w2[ab * 3 + c].astype(F32) for c in range(3)], axis=1) for ab in range(9)], axis=0
    )
    lhs2 = jnp.transpose(lhs2).astype(BF16)
    lhs3 = jnp.concatenate(
        [
            jnp.concatenate([w2[(8 - ab) * 3 + 2 - c].astype(F32) for ab in range(9)], axis=1)
            for c in range(3)
        ],
        axis=0,
    ).astype(BF16)
    bias1 = jnp.transpose(jnp.broadcast_to(b1[...], (nx, cone)))
    bias2 = jnp.transpose(jnp.broadcast_to(b2[...], (nx, ctwo)))
    lane1 = lax.broadcasted_iota(jnp.int32, (cone, nx), 1)
    lane2 = lax.broadcasted_iota(jnp.int32, (ctwo, nx), 1)

    def right(t, lane):
        return jnp.where(lane == 0, 0.0, pltpu.roll(t, 1, 1))

    def left(t, lane):
        return jnp.where(lane == nx - 1, 0.0, pltpu.roll(t, nx - 1, 1))

    for z in range(planes):
        for a in range(3):
            for b, y in ((0, 0), (2, ny - 1)):
                lanes = pl.ds((z * ny + y) * nx, nx)
                stack_a[pl.ds((a * 3 + b) * cone, cone), lanes] = jnp.zeros((cone, nx), BF16)
                stack_s[pl.ds((a * 3 + b) * ctwo, ctwo), lanes] = jnp.zeros((ctwo, nx), BF16)
    stack_a[pl.ds(9 * cone, 16), :] = jnp.ones((16, cells), BF16)
    for z in range(wide):
        for a in range(3):
            for b, y in ((0, 0), (2, ny - 1)):
                stack_v[pl.ds((a * 3 + b) * 8, 8), pl.ds((z * ny + y) * nx, nx)] = zero8

    has_lo = de > 0
    has_hi = de < nd - 1
    pl.semaphore_wait(bar, n - 1)

    def vol_copy(up):
        src = vol.at[:, pl.ds(planes - 2, 2)] if up else vol.at[:, pl.ds(0, 2)]
        side = 0 if up else 1
        return pltpu.make_async_remote_copy(
            src_ref=src, dst_ref=vrecv.at[side], send_sem=vs_sem.at[side], recv_sem=vr_sem.at[side],
            device_id=(dp, de + 1 if up else de - 1), device_id_type=MESH)

    def slope_copy(up):
        src = sl.at[planes - 1] if up else sl.at[0]
        side = 0 if up else 1
        return pltpu.make_async_remote_copy(
            src_ref=src, dst_ref=srecv.at[side], send_sem=ss_sem.at[side], recv_sem=sr_sem.at[side],
            device_id=(dp, de + 1 if up else de - 1), device_id_type=MESH)

    @pl.when(has_hi)
    def _():
        vol_copy(True).start()

    @pl.when(has_lo)
    def _():
        vol_copy(False).start()

    for side, has, z0 in ((0, has_lo, 0), (1, has_hi, planes + 2)):
        @pl.when(has)
        def _(side=side, z0=z0):
            vol_copy(side == 0).wait_recv()
            for ch in range(cin):
                for z in range(2):
                    v32[pl.ds((ch * wz + z0 + z) * ny, ny), :] = vrecv[side, ch, z].astype(F32)

        @pl.when(jnp.logical_not(has))
        def _(z0=z0):
            for ch in range(cin):
                for z in range(2):
                    v32[pl.ds((ch * wz + z0 + z) * ny, ny), :] = zero8

    row8 = lax.broadcasted_iota(jnp.int32, (8, nx), 0)
    for zz in range(wz):
        for y in range(ny):
            tile = v32[pl.ds(zz * ny + y, 8, stride=wz * ny), :]
            for a in range(3):
                z = zz - a
                if not 0 <= z < wide:
                    continue
                for b in range(3):
                    yo = y + 1 - b
                    if not 0 <= yo < ny:
                        continue
                    t = jnp.where(row8 == cin, 1.0, tile) if (a == 1 and b == 1) else tile
                    stack_v[pl.ds((a * 3 + b) * 8, 8), pl.ds((z * ny + yo) * nx, nx)] = t

    for zz in range(wide):
        res[pl.ds(0, 3 * cone), pl.ds(0, plane)] = jnp.dot(
            lhs1, stack_v[:, pl.ds(zz * plane, plane)].astype(BF16), preferred_element_type=F32)
        for y in range(ny):
            lanes = pl.ds(y * nx, nx)
            pre = (right(res[pl.ds(0, cone), lanes], lane1) + res[pl.ds(cone, cone), lanes]
                   + left(res[pl.ds(2 * cone, cone), lanes], lane1) + bias1)
            s = 1.0 / (1.0 + jnp.exp(-pre))
            act = pre * s
            if 1 <= zz <= planes:
                d_one[:, pl.ds(((zz - 1) * ny + y) * nx, nx)] = s * (1.0 + pre * (1.0 - s))
            elif zz == 0:
                act = jnp.where(has_lo, act, 0.0)
            else:
                act = jnp.where(has_hi, act, 0.0)
            act = act.astype(BF16)
            for a in range(3):
                z = zz - a
                if not 0 <= z < planes:
                    continue
                for b in range(3):
                    yo = y + 1 - b
                    if 0 <= yo < ny:
                        stack_a[pl.ds((a * 3 + b) * cone, cone), pl.ds((z * ny + yo) * nx, nx)] = act

    for z in range(planes):
        res[...] = jnp.dot(lhs2, stack_a[pl.ds(0, 9 * cone), pl.ds(z * plane, plane)], preferred_element_type=F32)
        for y in range(ny):
            lanes = pl.ds(y * nx, nx)
            pre = (right(res[pl.ds(0, ctwo), lanes], lane2) + res[pl.ds(ctwo, ctwo), lanes]
                   + left(res[pl.ds(2 * ctwo, ctwo), lanes], lane2) + bias2)
            s = 1.0 / (1.0 + jnp.exp(-pre))
            feat32[pl.ds(z * ny + y, ctwo, stride=planes * ny), :] = pre * s
            up = cot32[pl.ds(z * ny + y, ctwo, stride=planes * ny), :]
            slope = (up * (s * (1.0 + pre * (1.0 - s)))).astype(BF16)
            sl[z, :, lanes] = slope
            slf = slope.astype(F32)
            cell = pl.ds((z * ny + y) * nx, nx)
            slope3[pl.ds(0, ctwo), cell] = left(slf, lane2).astype(BF16)
            slope3[pl.ds(ctwo, ctwo), cell] = slope
            slope3[pl.ds(2 * ctwo, ctwo), cell] = right(slf, lane2).astype(BF16)
            for a in range(3):
                zo = z + 1 - a
                if not 0 <= zo < planes:
                    continue
                for b in range(3):
                    yo = y + 1 - b
                    if 0 <= yo < ny:
                        stack_s[pl.ds((a * 3 + b) * ctwo, ctwo), pl.ds((zo * ny + yo) * nx, nx)] = slope

    @pl.when(has_hi)
    def _():
        slope_copy(True).start()

    @pl.when(has_lo)
    def _():
        slope_copy(False).start()

    g2 = lax.dot_general(stack_a[...], slope3[...], NT, preferred_element_type=F32)
    k2 = 9 * cone
    last = g2[0:k2, 2 * ctwo:3 * ctwo]
    sb[pl.ds(0, k2 // ROWS)] = g2[0:k2, 0:2 * ctwo].astype(BF16).reshape(k2 // ROWS, ROWS, nx)
    sb[pl.ds(k2 // ROWS, k2 // 2 // ROWS)] = jnp.concatenate(
        [last[0:k2 // 2], last[k2 // 2:k2]], axis=1).astype(BF16).reshape(k2 // 2 // ROWS, ROWS, nx)
    b2row = g2[k2:k2 + 8, 0:2 * ctwo]
    feat[...] = feat32[...].reshape(feat.shape).astype(BF16)

    def shard_copy(s):
        owner = s * stride
        slot = lax.rem(me - owner + n, n) - 1
        return pltpu.make_async_remote_copy(
            src_ref=sb.at[s], dst_ref=rb.at[slot], send_sem=p1s, recv_sem=p1r,
            device_id=dev(owner), device_id_type=MESH)

    mine = lax.div(me, stride)
    is_owner = lax.rem(me, stride) == 0

    @pl.loop(0, nsh)
    def _(d):
        s = lax.rem(mine + d, nsh)

        @pl.when((s < early) & (s * stride != me))
        def _():
            shard_copy(s).start()

    for side, has, a, z in ((0, has_lo, 0, 0), (1, has_hi, 2, planes - 1)):
        @pl.when(has)
        def _(side=side):
            slope_copy(side == 0).wait_recv()

        @pl.when(jnp.logical_not(has))
        def _(side=side):
            srecv[side] = jnp.zeros((ctwo, plane), BF16)

        for y in range(ny):
            tile = srecv[side, :, pl.ds(y * nx, nx)]
            for b in range(3):
                yo = y + 1 - b
                if 0 <= yo < ny:
                    stack_s[pl.ds((a * 3 + b) * ctwo, ctwo), pl.ds((z * ny + yo) * nx, nx)] = tile

    for z in range(planes):
        res[pl.ds(0, 3 * cone), :] = jnp.dot(
            lhs3, stack_s[:, pl.ds(z * plane, plane)], preferred_element_type=F32)
        for y in range(ny):
            lanes = pl.ds(y * nx, nx)
            cell = pl.ds((z * ny + y) * nx, nx)
            back = (right(res[pl.ds(0, cone), lanes], lane1) + res[pl.ds(cone, cone), lanes]
                    + left(res[pl.ds(2 * cone, cone), lanes], lane1))
            slope = (back * d_one[:, cell]).astype(BF16)
            slf = slope.astype(F32)
            slope31[pl.ds(0, cone), cell] = left(slf, lane1).astype(BF16)
            slope31[pl.ds(cone, cone), cell] = slope
            slope31[pl.ds(2 * cone, cone), cell] = right(slf, lane1).astype(BF16)

    g1 = lax.dot_general(stack_v[:, pl.ds(plane, cells)].astype(BF16), slope31[...], NT, preferred_element_type=F32)
    g1 = jnp.concatenate([g1, jnp.zeros((72, nx - 3 * cone), F32)], axis=1)
    sb[pl.ds(early, nsh - early)] = jnp.concatenate([g1, b2row], axis=0).astype(BF16).reshape(nsh - early, ROWS, nx)

    @pl.loop(early, nsh)
    def _(s):
        @pl.when(s * stride != me)
        def _():
            shard_copy(s).start()

    def out_copy(t):
        return pltpu.make_async_remote_copy(
            src_ref=red, dst_ref=gath.at[mine], send_sem=p2s, recv_sem=p2r,
            device_id=dev(t), device_id_type=MESH)

    def drain(buf, sem):
        pltpu.make_async_copy(buf, buf, sem).wait()

    @pl.when(is_owner)
    def _():
        drain(rb, p1r)
        total = sb[mine].astype(F32) + jnp.sum(rb[...].astype(F32), axis=0)
        red[...] = total.astype(BF16)
        gath[mine] = total.astype(BF16)

        @pl.loop(1, n)
        def _(d):
            out_copy(lax.rem(me + d, n)).start()

        drain(gath.at[pl.ds(0, nsh - 1)], p2r)
        drain(sb.at[pl.ds(0, nsh - 1)], p1s)

    if stride > 1:
        @pl.when(jnp.logical_not(is_owner))
        def _():
            drain(gath, p2r)
            drain(sb, p1s)

    full = gath[...].reshape(nsh * ROWS, nx).astype(F32)
    for ab in range(9):
        r = ab * cone
        g2_o[ab * 3] = full[r:r + cone, 0:ctwo]
        g2_o[ab * 3 + 1] = full[r:r + cone, ctwo:2 * ctwo]
    half = k2 // 2
    tail = jnp.concatenate([full[k2:k2 + half, 0:ctwo], full[k2:k2 + half, ctwo:2 * ctwo]], axis=0)
    for ab in range(9):
        g2_o[ab * 3 + 2] = tail[ab * cone:(ab + 1) * cone]
    base = early * ROWS
    for ab in range(9):
        for c in range(3):
            g1_o[ab * 3 + c] = full[base + ab * 8:base + ab * 8 + cin, c * cone:(c + 1) * cone]
    gb1_o[...] = full[base + 4 * 8 + cin:base + 4 * 8 + cin + 1, cone:2 * cone]
    gb2_o[...] = full[base + 72:base + 73, ctwo:2 * ctwo]

    @pl.when(has_hi)
    def _():
        vol_copy(True).wait_send()
        slope_copy(True).wait_send()

    @pl.when(has_lo)
    def _():
        vol_copy(False).wait_send()
        slope_copy(False).wait_send()

    @pl.when(is_owner)
    def _():
        @pl.loop(1, n)
        def _(d):
            out_copy(lax.rem(me + d, n)).wait_send()


def per_device(n, nd, volume, kernel_one, bias_one, kernel_two, bias_two, cotangent):
    _, cin, planes, ny, nx = volume.shape
    cone, ctwo = kernel_one.shape[0], kernel_two.shape[0]
    cells = planes * ny * nx
    nsh = (27 * cone * ctwo // nx + 80) // ROWS
    w1 = jnp.transpose(kernel_one, (2, 3, 4, 1, 0)).reshape(27, cin, cone)
    w2 = jnp.transpose(kernel_two, (2, 3, 4, 1, 0)).reshape(27, cone, ctwo)
    vm = pl.BlockSpec(memory_space=pltpu.VMEM)
    dma = pltpu.SemaphoreType.DMA
    outs = pl.pallas_call(
        functools.partial(kernel, n, nd),
        out_shape=(
            jax.ShapeDtypeStruct((ctwo, planes, ny, nx), BF16),
            jax.ShapeDtypeStruct((27, cin, cone), F32),
            jax.ShapeDtypeStruct((1, cone), F32),
            jax.ShapeDtypeStruct((27, cone, ctwo), F32),
            jax.ShapeDtypeStruct((1, ctwo), F32),
        ),
        in_specs=[vm] * 6,
        out_specs=[vm] * 5,
        scratch_shapes=[
            pltpu.VMEM((2, cin, 2, ny, nx), BF16),
            pltpu.VMEM((8 * (planes + 4) * ny, nx), F32),
            pltpu.VMEM((72, (planes + 2) * ny * nx), F32),
            pltpu.VMEM((ctwo * planes * ny, nx), F32),
            pltpu.VMEM((cone, cells), F32),
            pltpu.VMEM((9 * cone + 16, cells), BF16),
            pltpu.VMEM((3 * ctwo, ny * nx), F32),
            pltpu.VMEM((3 * ctwo, cells), BF16),
            pltpu.VMEM((planes, ctwo, ny * nx), BF16),
            pltpu.VMEM((2, ctwo, ny * nx), BF16),
            pltpu.VMEM((9 * ctwo, cells), BF16),
            pltpu.VMEM((ctwo * planes * ny, nx), F32),
            pltpu.VMEM((3 * cone, cells), BF16),
            pltpu.VMEM((nsh, ROWS, nx), BF16),
            pltpu.VMEM((n - 1, ROWS, nx), BF16),
            pltpu.VMEM((ROWS, nx), BF16),
            pltpu.VMEM((nsh, ROWS, nx), BF16),
            dma((2,)), dma((2,)), dma((2,)), dma((2,)),
            dma, dma, dma, dma,
        ],
        compiler_params=pltpu.CompilerParams(
            collective_id=0, has_side_effects=True, vmem_limit_bytes=48 * 1024 * 1024),
    )(
        volume.reshape(cin, planes, ny, nx), w1, bias_one.reshape(1, cone), w2,
        bias_two.reshape(1, ctwo), cotangent.reshape(ctwo, planes, ny, nx),
    )
    feat, g1, gb1, g2, gb2 = outs
    g1 = jnp.transpose(g1.reshape(3, 3, 3, cin, cone), (4, 3, 0, 1, 2))
    g2 = jnp.transpose(g2.reshape(3, 3, 3, cone, ctwo), (4, 3, 0, 1, 2))
    return feat[None], g1, gb1.reshape(cone), g2, gb2.reshape(ctwo)


def solution(mesh):
    nd = mesh.shape["depth"]
    n = mesh.shape["dp"] * nd
    return jax.shard_map(
        functools.partial(per_device, n, nd),
        mesh=mesh,
        in_specs=(
            P("dp", None, "depth", None, None),
            P(),
            P(),
            P(),
            P(),
            P("dp", None, "depth", None, None),
        ),
        out_specs=(P("dp", None, "depth", None, None), P(), P(), P(), P()),
        check_vma=False,
    )
```

time: 181 us -> 35.3 us (0.20)
  waiting for transfers between devices: 62.6 us -> 0 us
  blocking collectives: 43.4 us -> 0 us
  Pallas kernels: 0 us -> 27.2 us
  matrix products: 22.5 us -> 0 us
  local copies, waits for them, and re-layouts: 23.7 us -> 7.11 us
  between operations: 14.4 us -> 0.66 us
  starting transfers between devices: 10.1 us -> 0 us
  other arithmetic: 3.68 us -> 0 us
    psum x1 -> x0, waiting for transfers between devices: 59.5 us -> none  [per_device(): lax.psum((grad_one, bias_grad_one, grad_two, bias_grad_two), ('dp', 'dept...]
    psum x1 -> x0, blocking collectives: 43.4 us -> none  [per_device(): lax.psum((grad_one, bias_grad_one, grad_two, bias_grad_two), ('dp', 'dept...]
    pallas_call x0 -> x1, Pallas kernels: none -> 27.2 us  [per_device(): pl.pallas_call(functools.partial(kernel, n, nd), out_shape=(jax.ShapeDtyp...]
    conv_general_dilated x5 -> x0, matrix products: 22.5 us -> none  [the longest x3 13.9 us: convolve(): lax.conv_general_dilated(inputs, kernel, (1, 1, 1), ((depth_pad, depth_pa...]
    ppermute x4 -> x0, starting transfers between devices: 10.1 us -> none  [the longest x2 7.52 us: extended(): before = lax.ppermute(last, axis, up)]
    concatenate x7 -> x0, local copies, waits for them, and re-layouts: 5.95 us -> none  [extended(): x = jnp.concatenate([before, x, after], axis=dim)]
    unnamed x35 -> x17, local copies, waits for them, and re-layouts: 11.6 us -> 7.11 us
    ppermute x4 -> x0, waiting for transfers between devices: 3.11 us -> none  [the longest x2 3.1 us: extended(): after = lax.ppermute(leading, axis, down)]
  transfers between devices with their start and end apart: 5 -> 0, of which waited for: 2 -> 0; matrix products, arithmetic and copies ran while one was open for 12% -> 0% of each run, Pallas kernels for 0% -> 0%
where the time goes in v1:
time: 35.3 us; the launch traced here: 35 us
  Pallas kernels  27.2 us (77%)
  local copies, waits for them, and re-layouts  7.11 us (20%)
  between operations  0.66 us (2%)
    pallas_call x1, Pallas kernels, per_device(): pl.pallas_call(functools.partial(kernel, n, nd), out_shape=(jax.ShapeDtyp...  27.2 us
    unnamed x17, local copies, waits for them, and re-layouts  7.11 us

profile of v1, /device:TPU:0, one launch (start us, length us, event | category | flops | bytes accessed | tf_op | source)
XLA Modules:
  0.0 35.0 jit_solution(14519330678448992593)
XLA Ops:
  0.6 0.0 copy-start.4
  0.6 0.0 copy-start.5
  0.7 0.6 %copy-done.4 = f32[32]{0:T(128)S(1)} copy-done((f32[32]{0:T(128)S(1)}, f32[32]{0:T(128)}, u32[]{:S(2)}) %copy-start.4) | copy-done | bytes 152
  1.3 0.0 copy-done.5
  1.3 0.0 copy-start
  1.3 0.9 %copy-done = bf16[1,64,2,8,128]{4,3,2,1,0:T(8,128)(2,1)S(1)} copy-done((bf16[1,64,2,8,128]{4,3,2,1,0:T(8,128)(2,1)S(1)}, bf16[1,64,2,8,128]{4,3,2,1,0:T(8,128)(2,1)}, u32[]{:S(2)}) %copy-start) | copy-done | bytes 262168
  2.3 0.0 copy-start.1
  2.3 0.9 %copy-done.1 = bf16[64,32,3,3,3]{0,1,4,3,2:T(8,128)(2,1)S(1)} copy-done((bf16[64,32,3,3,3]{0,1,4,3,2:T(8,128)(2,1)S(1)}, bf16[64,32,3,3,3]{0,1,4,3,2:T(8,128)(2,1)}, u32[]{:S(2)}) %copy-start.1) | copy-done | bytes 110616
  3.2 0.0 copy-start.2
  3.2 0.7 %copy-done.2 = bf16[32,4,3,3,3]{0,1,4,3,2:T(4,128)(2,1)S(1)} copy-done((bf16[32,4,3,3,3]{0,1,4,3,2:T(4,128)(2,1)S(1)}, bf16[32,4,3,3,3]{0,1,4,3,2:T(4,128)(2,1)}, u32[]{:S(2)}) %copy-start.2) | copy-done | bytes 6936
  3.9 0.0 copy-start.3
  3.9 0.7 %copy-done.3 = bf16[1,4,2,8,128]{4,3,2,1,0:T(8,128)(2,1)S(1)} copy-done((bf16[1,4,2,8,128]{4,3,2,1,0:T(8,128)(2,1)S(1)}, bf16[1,4,2,8,128]{4,3,2,1,0:T(8,128)(2,1)}, u32[]{:S(2)}) %copy-start.3) | copy-done | bytes 16408
  4.7 27.2 %shard_map.101 = (bf16[64,2,8,128]{3,2,1,0:T(8,128)(2,1)S(1)}, f32[27,4,32]{2,1,0:T(4,128)S(1)}, f32[1,32]{1,0:T(1,128)S(1)}, f32[27,32,64]{2,1,0:T(8,128)S(1)}, f32[1,64]{1,0:T(1,128)S(1)}) custom-call(bf16[4,2,8,128]{3,2,1,0:T(8,128)(2,1)S(1)} %bitcast.25, bf16[27,4,32]{2,1,0:T(4,128)(2,1)S(1)} %bitcast.24, f32[1,32]{1,0:T(1,128)S(1)} %bitcast.26, ...), custom_call_target="tpu_custom_call" | custom-call | tf_op jit(solution)/shard_map/pallas_call | solution.py:341
  31.9 0.7 %copy.16 = bf16[1,64,2,8,128]{4,3,2,1,0:T(8,128)(2,1)} copy(bf16[1,64,2,8,128]{4,3,2,1,0:T(8,128)(2,1)S(1)} %bitcast.21) | data formatting | bytes 524288
  32.6 0.6 %copy.17 = f32[32,4,3,3,3]{0,1,4,3,2:T(4,128)} copy(f32[32,4,3,3,3]{0,1,4,3,2:T(4,128)S(1)} %bitcast.23) | data formatting | bytes 27648
  33.2 0.5 %copy.18 = f32[32]{0:T(128)} copy(f32[32]{0:T(128)S(1)} %bitcast.29) | data formatting | bytes 256
  33.7 0.8 %copy.19 = f32[64,32,3,3,3]{0,1,4,3,2:T(8,128)} copy(f32[64,32,3,3,3]{0,1,4,3,2:T(8,128)S(1)} %bitcast.19) | data formatting | bytes 442368
  34.5 0.5 %copy.20 = f32[64]{0:T(128)} copy(f32[64]{0:T(128)S(1)} %bitcast.28) | data formatting | bytes 512
Async XLA Ops:
  0.6 0.7 %copy-start.4 = (f32[32]{0:T(128)S(1)}, f32[32]{0:T(128)}, u32[]{:S(2)}) copy-start(f32[32]{0:T(128)} %param.8) | copy-start | bytes 388
  0.6 0.7 %copy-start.5 = (f32[64]{0:T(128)S(1)}, f32[64]{0:T(128)}, u32[]{:S(2)}) copy-start(f32[64]{0:T(128)} %param.10) | copy-start | bytes 772
  1.3 0.9 %copy-start = (bf16[1,64,2,8,128]{4,3,2,1,0:T(8,128)(2,1)S(1)}, bf16[1,64,2,8,128]{4,3,2,1,0:T(8,128)(2,1)}, u32[]{:S(2)}) copy-start(bf16[1,64,2,8,128]{4,3,2,1,0:T(8,128)(2,1)} %param.11) | copy-start | bytes 786436
  2.3 0.9 %copy-start.1 = (bf16[64,32,3,3,3]{0,1,4,3,2:T(8,128)(2,1)S(1)}, bf16[64,32,3,3,3]{0,1,4,3,2:T(8,128)(2,1)}, u32[]{:S(2)}) copy-start(bf16[64,32,3,3,3]{0,1,4,3,2:T(8,128)(2,1)} %param.9) | copy-start | bytes 331780
  3.2 0.7 %copy-start.2 = (bf16[32,4,3,3,3]{0,1,4,3,2:T(4,128)(2,1)S(1)}, bf16[32,4,3,3,3]{0,1,4,3,2:T(4,128)(2,1)}, u32[]{:S(2)}) copy-start(bf16[32,4,3,3,3]{0,1,4,3,2:T(4,128)(2,1)} %param.7) | copy-start | bytes 20740
  3.9 0.7 %copy-start.3 = (bf16[1,4,2,8,128]{4,3,2,1,0:T(8,128)(2,1)S(1)}, bf16[1,4,2,8,128]{4,3,2,1,0:T(8,128)(2,1)}, u32[]{:S(2)}) copy-start(bf16[1,4,2,8,128]{4,3,2,1,0:T(8,128)(2,1)} %param.6) | copy-start | bytes 49156

commit v2 on v1

--- a/solution.py
+++ b/solution.py
@@ -10,45 +10,62 @@
 F32 = jnp.float32
 BF16 = jnp.bfloat16
 MESH = pl.DeviceIdType.MESH
-ROWS = 16
+INNER = 4
 NT = (((1,), (1,)), ((), ()))
 
 
-def kernel(n, nd, vol, w1, b1, w2, b2, cot, feat, g1_o, gb1_o, g2_o, gb2_o,
+def kernel(ni, nz, nd, vol_h, w1_h, b1_h, w2_h, b2_h, cot_h, feat, packed,
+           vol, w1, b1, w2, b2, cot,
            vrecv, v32, stack_v, cot32, d_one, stack_a, res, slope3, sl, srecv,
-           stack_s, feat32, slope31, sb, rb, red, gath,
-           vs_sem, vr_sem, ss_sem, sr_sem, p1s, p1r, p2s, p2r):
+           stack_s, feat32, slope31, sb, rb, zb, zsrc, gath,
+           in_sem, vs_sem, vr_sem, ss_sem, sr_sem, p1s, p1r, pzs, pzr, p2s, p2r):
     cin, planes, ny, nx = vol.shape
     cone, ctwo = w2.shape[1], w2.shape[2]
     cells = planes * ny * nx
     plane = ny * nx
     wide = planes + 2
-    nsh = sb.shape[0]
-    stride = n // nsh
-    early = (27 * cone * ctwo // nx) // ROWS
+    nsh, rows = sb.shape[0], sb.shape[1]
+    early = (27 * cone * ctwo // nx) // rows
 
     de = lax.axis_index("depth")
-    me = lax.axis_index("dp") * nd + de
     dp = lax.axis_index("dp")
-
-    def dev(t):
-        return (lax.div(t, nd), lax.rem(t, nd))
+    zi = lax.div(dp, ni)
+    me = lax.rem(dp, ni) * nd + de
+
+    loads = [
+        pltpu.make_async_copy(src, dst, in_sem.at[i])
+        for i, (src, dst) in enumerate(
+            ((vol_h, vol), (w1_h, w1), (b1_h, b1), (w2_h, w2), (b2_h, b2), (cot_h, cot)))
+    ]
+    for copy in loads:
+        copy.start()
+
+    def peer(j):
+        return (zi * ni + lax.div(j, nd), lax.rem(j, nd))
+
+    def column(k):
+        return (k * ni + lax.rem(dp, ni), de)
 
     bar = pltpu.get_barrier_semaphore()
 
-    @pl.loop(1, n)
+    @pl.loop(1, nsh)
     def _(d):
-        pl.semaphore_signal(bar, inc=1, device_id=dev(lax.rem(me + d, n)), device_id_type=MESH)
-
-    cot32[...] = cot[...].astype(F32).reshape(cot32.shape)
+        pl.semaphore_signal(bar, inc=1, device_id=peer(lax.rem(me + d, nsh)), device_id_type=MESH)
+
+    for d in range(1, nz):
+        pl.semaphore_signal(bar, inc=1, device_id=column(lax.rem(zi + d, nz)), device_id_type=MESH)
+
     wz = planes + 4
     zero8 = jnp.zeros((ny, nx), F32)
+    loads[0].wait()
     for ch in range(8):
         for z in range(planes if ch < cin else wz):
             if ch < cin:
                 v32[pl.ds((ch * wz + z + 2) * ny, ny), :] = vol[ch, z].astype(F32)
             else:
                 v32[pl.ds((ch * wz + z) * ny, ny), :] = zero8
+    for copy in loads[1:5]:
+        copy.wait()
     lhs1 = []
     for ab in range(9):
         row = jnp.concatenate([w1[ab * 3 + c].astype(F32) for c in range(3)], axis=1)
@@ -88,9 +105,11 @@
             for b, y in ((0, 0), (2, ny - 1)):
                 stack_v[pl.ds((a * 3 + b) * 8, 8), pl.ds((z * ny + y) * nx, nx)] = zero8
 
+    loads[5].wait()
+    cot32[...] = cot[...].astype(F32).reshape(cot32.shape)
     has_lo = de > 0
     has_hi = de < nd - 1
-    pl.semaphore_wait(bar, n - 1)
+    pl.semaphore_wait(bar, nsh - 1 + nz - 1)
 
     def vol_copy(up):
         src = vol.at[:, pl.ds(planes - 2, 2)] if up else vol.at[:, pl.ds(0, 2)]
@@ -204,27 +223,23 @@
     g2 = lax.dot_general(stack_a[...], slope3[...], NT, preferred_element_type=F32)
     k2 = 9 * cone
     last = g2[0:k2, 2 * ctwo:3 * ctwo]
-    sb[pl.ds(0, k2 // ROWS)] = g2[0:k2, 0:2 * ctwo].astype(BF16).reshape(k2 // ROWS, ROWS, nx)
-    sb[pl.ds(k2 // ROWS, k2 // 2 // ROWS)] = jnp.concatenate(
-        [last[0:k2 // 2], last[k2 // 2:k2]], axis=1).astype(BF16).reshape(k2 // 2 // ROWS, ROWS, nx)
+    tail = jnp.concatenate([last[0:k2 // 2], last[k2 // 2:k2]], axis=1).astype(BF16)
+    cut = early * rows - k2
+    sb[pl.ds(0, early)] = jnp.concatenate(
+        [g2[0:k2, 0:2 * ctwo].astype(BF16), tail[0:cut]], axis=0).reshape(early, rows, nx)
     b2row = g2[k2:k2 + 8, 0:2 * ctwo]
-    feat[...] = feat32[...].reshape(feat.shape).astype(BF16)
 
     def shard_copy(s):
-        owner = s * stride
-        slot = lax.rem(me - owner + n, n) - 1
+        slot = lax.rem(me - s + nsh, nsh) - 1
         return pltpu.make_async_remote_copy(
             src_ref=sb.at[s], dst_ref=rb.at[slot], send_sem=p1s, recv_sem=p1r,
-            device_id=dev(owner), device_id_type=MESH)
-
-    mine = lax.div(me, stride)
-    is_owner = lax.rem(me, stride) == 0
-
-    @pl.loop(0, nsh)
+            device_id=peer(s), device_id_type=MESH)
+
+    @pl.loop(1, nsh)
     def _(d):
-        s = lax.rem(mine + d, nsh)
-
-        @pl.when((s < early) & (s * stride != me))
+        s = lax.rem(me + d, nsh)
+
+        @pl.when(s < early)
         def _():
             shard_copy(s).start()
 
@@ -260,96 +275,122 @@
 
     g1 = lax.dot_general(stack_v[:, pl.ds(plane, cells)].astype(BF16), slope31[...], NT, preferred_element_type=F32)
     g1 = jnp.concatenate([g1, jnp.zeros((72, nx - 3 * cone), F32)], axis=1)
-    sb[pl.ds(early, nsh - early)] = jnp.concatenate([g1, b2row], axis=0).astype(BF16).reshape(nsh - early, ROWS, nx)
+    late = jnp.concatenate([g1, b2row], axis=0).astype(BF16)
+    if cut < tail.shape[0]:
+        late = jnp.concatenate([tail[cut:], late], axis=0)
+    sb[pl.ds(early, nsh - early)] = late.reshape(nsh - early, rows, nx)
 
     @pl.loop(early, nsh)
     def _(s):
-        @pl.when(s * stride != me)
+        @pl.when(s != me)
         def _():
             shard_copy(s).start()
 
-    def out_copy(t):
-        return pltpu.make_async_remote_copy(
-            src_ref=red, dst_ref=gath.at[mine], send_sem=p2s, recv_sem=p2r,
-            device_id=dev(t), device_id_type=MESH)
-
     def drain(buf, sem):
         pltpu.make_async_copy(buf, buf, sem).wait()
 
-    @pl.when(is_owner)
-    def _():
-        drain(rb, p1r)
-        total = sb[mine].astype(F32) + jnp.sum(rb[...].astype(F32), axis=0)
-        red[...] = total.astype(BF16)
-        gath[mine] = total.astype(BF16)
-
-        @pl.loop(1, n)
-        def _(d):
-            out_copy(lax.rem(me + d, n)).start()
-
-        drain(gath.at[pl.ds(0, nsh - 1)], p2r)
-        drain(sb.at[pl.ds(0, nsh - 1)], p1s)
-
-    if stride > 1:
-        @pl.when(jnp.logical_not(is_owner))
-        def _():
-            drain(gath, p2r)
-            drain(sb, p1s)
-
-    full = gath[...].reshape(nsh * ROWS, nx).astype(F32)
+    drain(rb, p1r)
+    total = (sb[me].astype(F32) + jnp.sum(rb[...].astype(F32), axis=0)).astype(BF16)
+    zsrc[...] = total
+    zb[zi] = total
+
+    def z_copy(d):
+        return pltpu.make_async_remote_copy(
+            src_ref=zsrc, dst_ref=zb.at[zi], send_sem=pzs, recv_sem=pzr,
+            device_id=column(lax.rem(zi + d, nz)), device_id_type=MESH)
+
+    for d in range(1, nz):
+        z_copy(d).start()
+    feat[...] = feat32[...].reshape(feat.shape).astype(BF16)
+    drain(zb.at[pl.ds(0, nz - 1)], pzr)
+    whole = zb[0].astype(F32)
+    for k in range(1, nz):
+        whole = whole + zb[k].astype(F32)
+    gath[me] = whole.astype(BF16)
+
+    def out_copy(d):
+        return pltpu.make_async_remote_copy(
+            src_ref=gath.at[me], dst_ref=gath.at[me], send_sem=p2s, recv_sem=p2r,
+            device_id=peer(lax.rem(me + d, nsh)), device_id_type=MESH)
+
+    @pl.loop(1, nsh)
+    def _(d):
+        out_copy(d).start()
+
+    drain(gath.at[pl.ds(0, nsh - 1)], p2r)
+    packed[...] = gath[...].reshape(packed.shape)
+
+    drain(sb.at[pl.ds(0, nsh - 1)], p1s)
+    drain(zb.at[pl.ds(0, nz - 1)], pzs)
+    drain(gath.at[pl.ds(0, nsh - 1)], p2s)
+
+    @pl.when(has_hi)
+    def _():
+        vol_copy(True).wait_send()
+        slope_copy(True).wait_send()
+
+    @pl.when(has_lo)
+    def _():
+        vol_copy(False).wait_send()
+        slope_copy(False).wait_send()
+
+
+def unpack(feat, packed, feat_o, g1_o, gb1_o, g2_o, gb2_o, g1, gb1, g2, gb2, sem):
+    cin, cone, ctwo = g1.shape[1], g2.shape[1], g2.shape[2]
+    k2 = 9 * cone
+    half = k2 // 2
+    base = k2 + half
+    first = pltpu.make_async_copy(feat, feat_o, sem.at[0])
+    first.start()
+    full = packed[...].astype(F32)
     for ab in range(9):
         r = ab * cone
-        g2_o[ab * 3] = full[r:r + cone, 0:ctwo]
-        g2_o[ab * 3 + 1] = full[r:r + cone, ctwo:2 * ctwo]
-    half = k2 // 2
-    tail = jnp.concatenate([full[k2:k2 + half, 0:ctwo], full[k2:k2 + half, ctwo:2 * ctwo]], axis=0)
+        g2[ab * 3] = full[r:r + cone, 0:ctwo]
+        g2[ab * 3 + 1] = full[r:r + cone, ctwo:2 * ctwo]
+    tail = jnp.concatenate([full[k2:base, 0:ctwo], full[k2:base, ctwo:2 * ctwo]], axis=0)
     for ab in range(9):
-        g2_o[ab * 3 + 2] = tail[ab * cone:(ab + 1) * cone]
-    base = early * ROWS
+        g2[ab * 3 + 2] = tail[ab * cone:(ab + 1) * cone]
+    copies = [first, pltpu.make_async_copy(g2, g2_o, sem.at[1])]
+    copies[1].start()
     for ab in range(9):
         for c in range(3):
-            g1_o[ab * 3 + c] = full[base + ab * 8:base + ab * 8 + cin, c * cone:(c + 1) * cone]
-    gb1_o[...] = full[base + 4 * 8 + cin:base + 4 * 8 + cin + 1, cone:2 * cone]
-    gb2_o[...] = full[base + 72:base + 73, ctwo:2 * ctwo]
-
-    @pl.when(has_hi)
-    def _():
-        vol_copy(True).wait_send()
-        slope_copy(True).wait_send()
-
-    @pl.when(has_lo)
-    def _():
-        vol_copy(False).wait_send()
-        slope_copy(False).wait_send()
-
-    @pl.when(is_owner)
-    def _():
-        @pl.loop(1, n)
-        def _(d):
-            out_copy(lax.rem(me + d, n)).wait_send()
-
-
-def per_device(n, nd, volume, kernel_one, bias_one, kernel_two, bias_two, cotangent):
+            g1[ab * 3 + c] = full[base + ab * 8:base + ab * 8 + cin, c * cone:(c + 1) * cone]
+    gb1[...] = full[base + 4 * 8 + cin:base + 4 * 8 + cin + 1, cone:2 * cone]
+    gb2[...] = full[base + 72:base + 73, ctwo:2 * ctwo]
+    for i, (src, dst) in enumerate(((g1, g1_o), (gb1, gb1_o), (gb2, gb2_o))):
+        copies.append(pltpu.make_async_copy(src, dst, sem.at[2 + i]))
+        copies[-1].start()
+    for copy in copies:
+        copy.wait()
+
+
+def per_device(ni, nz, nd, volume, kernel_one, bias_one, kernel_two, bias_two, cotangent):
     _, cin, planes, ny, nx = volume.shape
     cone, ctwo = kernel_one.shape[0], kernel_two.shape[0]
     cells = planes * ny * nx
-    nsh = (27 * cone * ctwo // nx + 80) // ROWS
+    total = 27 * cone * ctwo // nx + 80
+    nsh = ni * nd
+    rows = total // nsh
     w1 = jnp.transpose(kernel_one, (2, 3, 4, 1, 0)).reshape(27, cin, cone)
     w2 = jnp.transpose(kernel_two, (2, 3, 4, 1, 0)).reshape(27, cone, ctwo)
     vm = pl.BlockSpec(memory_space=pltpu.VMEM)
+    hbm = pl.BlockSpec(memory_space=pltpu.HBM)
     dma = pltpu.SemaphoreType.DMA
-    outs = pl.pallas_call(
-        functools.partial(kernel, n, nd),
+    feat, packed = pl.pallas_call(
+        functools.partial(kernel, ni, nz, nd),
         out_shape=(
             jax.ShapeDtypeStruct((ctwo, planes, ny, nx), BF16),
-            jax.ShapeDtypeStruct((27, cin, cone), F32),
-            jax.ShapeDtypeStruct((1, cone), F32),
-            jax.ShapeDtypeStruct((27, cone, ctwo), F32),
-            jax.ShapeDtypeStruct((1, ctwo), F32),
+            jax.ShapeDtypeStruct((total, nx), BF16),
         ),
-        in_specs=[vm] * 6,
-        out_specs=[vm] * 5,
+        in_specs=[hbm] * 6,
+        out_specs=[vm] * 2,
         scratch_shapes=[
+            pltpu.VMEM((cin, planes, ny, nx), BF16),
+            pltpu.VMEM((27, cin, cone), BF16),
+            pltpu.VMEM((1, cone), F32),
+            pltpu.VMEM((27, cone, ctwo), BF16),
+            pltpu.VMEM((1, ctwo), F32),
+            pltpu.VMEM((ctwo, planes, ny, nx), BF16),
             pltpu.VMEM((2, cin, 2, ny, nx), BF16),
             pltpu.VMEM((8 * (planes + 4) * ny, nx), F32),
             pltpu.VMEM((72, (planes + 2) * ny * nx), F32),
@@ -363,20 +404,33 @@
             pltpu.VMEM((9 * ctwo, cells), BF16),
             pltpu.VMEM((ctwo * planes * ny, nx), F32),
             pltpu.VMEM((3 * cone, cells), BF16),
-            pltpu.VMEM((nsh, ROWS, nx), BF16),
-            pltpu.VMEM((n - 1, ROWS, nx), BF16),
-            pltpu.VMEM((ROWS, nx), BF16),
-            pltpu.VMEM((nsh, ROWS, nx), BF16),
+            pltpu.VMEM((nsh, rows, nx), BF16),
+            pltpu.VMEM((nsh - 1, rows, nx), BF16),
+            pltpu.VMEM((nz, rows, nx), BF16),
+            pltpu.VMEM((rows, nx), BF16),
+            pltpu.VMEM((nsh, rows, nx), BF16),
+            dma((6,)),
             dma((2,)), dma((2,)), dma((2,)), dma((2,)),
-            dma, dma, dma, dma,
+            dma, dma, dma, dma, dma, dma,
         ],
         compiler_params=pltpu.CompilerParams(
             collective_id=0, has_side_effects=True, vmem_limit_bytes=48 * 1024 * 1024),
-    )(
-        volume.reshape(cin, planes, ny, nx), w1, bias_one.reshape(1, cone), w2,
-        bias_two.reshape(1, ctwo), cotangent.reshape(ctwo, planes, ny, nx),
-    )
-    feat, g1, gb1, g2, gb2 = outs
+    )(*(
+        pltpu.with_memory_space_constraint(x, pltpu.HBM)
+        for x in (
+            volume.reshape(cin, planes, ny, nx), w1, bias_one.reshape(1, cone), w2,
+            bias_two.reshape(1, ctwo), cotangent.reshape(ctwo, planes, ny, nx))
+    ))
+    shapes = (((ctwo, planes, ny, nx), BF16), ((27, cin, cone), F32), ((1, cone), F32),
+              ((27, cone, ctwo), F32), ((1, ctwo), F32))
+    feat, g1, gb1, g2, gb2 = pl.pallas_call(
+        unpack,
+        out_shape=tuple(jax.ShapeDtypeStruct(*x) for x in shapes),
+        in_specs=[vm] * 2,
+        out_specs=[hbm] * 5,
+        scratch_shapes=[pltpu.VMEM(*x) for x in shapes[1:]] + [dma((5,))],
+        compiler_params=pltpu.CompilerParams(vmem_limit_bytes=8 * 1024 * 1024),
+    )(feat, packed)
     g1 = jnp.transpose(g1.reshape(3, 3, 3, cin, cone), (4, 3, 0, 1, 2))
     g2 = jnp.transpose(g2.reshape(3, 3, 3, cone, ctwo), (4, 3, 0, 1, 2))
     return feat[None], g1, gb1.reshape(cone), g2, gb2.reshape(ctwo)
@@ -384,9 +438,10 @@
 
 def solution(mesh):
     nd = mesh.shape["depth"]
-    n = mesh.shape["dp"] * nd
+    ni = min(INNER, mesh.shape["dp"])
+    nz = mesh.shape["dp"] // ni
     return jax.shard_map(
-        functools.partial(per_device, n, nd),
+        functools.partial(per_device, ni, nz, nd),
         mesh=mesh,
         in_specs=(
             P("dp", None, "depth", None, None),

time: 35.3 us -> 27 us (0.76)
  local copies, waits for them, and re-layouts: 7.11 us -> 0 us
  Pallas kernels: 27.2 us -> 26.1 us
    unnamed x17 -> x0, local copies, waits for them, and re-layouts: 7.11 us -> none
    pallas_call x1 -> x2, Pallas kernels: 27.2 us -> 26.1 us  [the longest x1 25.2 us: per_device(): pl.pallas_call(functools.partial(kernel, ni, nz, nd), out_shape=(jax.Shap...]
where the time goes in v2:
time: 27 us; the launch traced here: 26.8 us
  Pallas kernels  26.1 us (97%)
  between operations  0.64 us (2%)
    pallas_call x1, Pallas kernels, per_device(): pl.pallas_call(functools.partial(kernel, ni, nz, nd), out_shape=(jax.Shap...  25.2 us
    pallas_call x1, Pallas kernels, per_device(): pl.pallas_call(unpack, out_shape=tuple((jax.ShapeDtypeStruct(*x) for x in...  0.92 us

profile of v2, /device:TPU:0, one launch (start us, length us, event | category | flops | bytes accessed | tf_op | source)
XLA Modules:
  0.0 26.8 jit_solution(18225323560395587758)
XLA Ops:
  0.6 25.2 %shard_map.101 = (bf16[64,2,8,128]{3,2,1,0:T(8,128)(2,1)S(1)}, bf16[512,128]{1,0:T(8,128)(2,1)S(1)}) custom-call(bf16[4,2,8,128]{3,2,1,0:T(8,128)(2,1)} %bitcast.22, bf16[27,4,32]{2,1,0:T(4,128)(2,1)} %bitcast.21, f32[1,32]{1,0:T(1,128)} %bitcast.23, bf16[27,32,64]{2,1,0:T(8,128)(2,1)} %bitcast.20, f32[1,64]{1,0:T(1,128)} %bitcast.24, ...), custom_call_target="tpu_custom_call" | custom-call | tf_op jit(solution)/shard_map/pallas_call | solution.py:379
  25.9 0.9 %shard_map.102 = (bf16[64,2,8,128]{3,2,1,0:T(8,128)(2,1)}, f32[27,4,32]{2,1,0:T(4,128)}, f32[1,32]{1,0:T(1,128)}, f32[27,32,64]{2,1,0:T(8,128)}, f32[1,64]{1,0:T(1,128)}) custom-call(bf16[64,2,8,128]{3,2,1,0:T(8,128)(2,1)S(1)} %get-tuple-element.12.feat, bf16[512,128]{1,0:T(8,128)(2,1)S(1)} %get-tuple-element.13.packed), custom_call_target="tpu_custom_call" | custom-call | tf_op jit(solution)/shard_map/pallas_call | solution.py:426

commit v3 on v2

--- a/solution.py
+++ b/solution.py
@@ -14,16 +14,22 @@
 NT = (((1,), (1,)), ((), ()))
 
 
+def halo_parts(planes, nd):
+    parts = ((1, 0, 3, 0),) if planes >= 3 else ((1, 1, 2, 0), (2, 0, 1, 2))
+    return tuple(p for p in parts if p[0] < nd)
+
+
 def kernel(ni, nz, nd, vol_h, w1_h, b1_h, w2_h, b2_h, cot_h, feat, packed,
            vol, w1, b1, w2, b2, cot,
-           vrecv, v32, stack_v, cot32, d_one, stack_a, res, slope3, sl, srecv,
+           vrecv, v32, stack_v, cot32, d_one, stack_a, res, slope3, crecv, ccot32,
            stack_s, feat32, slope31, sb, rb, zb, zsrc, gath,
            in_sem, vs_sem, vr_sem, ss_sem, sr_sem, p1s, p1r, pzs, pzr, p2s, p2r):
     cin, planes, ny, nx = vol.shape
     cone, ctwo = w2.shape[1], w2.shape[2]
     cells = planes * ny * nx
     plane = ny * nx
-    wide = planes + 2
+    wide = planes + 4
+    parts = halo_parts(planes, nd)
     nsh, rows = sb.shape[0], sb.shape[1]
     early = (27 * cone * ctwo // nx) // rows
 
@@ -55,13 +61,13 @@
     for d in range(1, nz):
         pl.semaphore_signal(bar, inc=1, device_id=column(lax.rem(zi + d, nz)), device_id_type=MESH)
 
-    wz = planes + 4
+    wz = planes + 6
     zero8 = jnp.zeros((ny, nx), F32)
     loads[0].wait()
     for ch in range(8):
         for z in range(planes if ch < cin else wz):
             if ch < cin:
-                v32[pl.ds((ch * wz + z + 2) * ny, ny), :] = vol[ch, z].astype(F32)
+                v32[pl.ds((ch * wz + z + 3) * ny, ny), :] = vol[ch, z].astype(F32)
             else:
                 v32[pl.ds((ch * wz + z) * ny, ny), :] = zero8
     for copy in loads[1:5]:
@@ -93,13 +99,14 @@
     def left(t, lane):
         return jnp.where(lane == nx - 1, 0.0, pltpu.roll(t, nx - 1, 1))
 
-    for z in range(planes):
+    for z in range(planes + 2):
         for a in range(3):
             for b, y in ((0, 0), (2, ny - 1)):
                 lanes = pl.ds((z * ny + y) * nx, nx)
                 stack_a[pl.ds((a * 3 + b) * cone, cone), lanes] = jnp.zeros((cone, nx), BF16)
-                stack_s[pl.ds((a * 3 + b) * ctwo, ctwo), lanes] = jnp.zeros((ctwo, nx), BF16)
-    stack_a[pl.ds(9 * cone, 16), :] = jnp.ones((16, cells), BF16)
+                if z < planes:
+                    stack_s[pl.ds((a * 3 + b) * ctwo, ctwo), lanes] = jnp.zeros((ctwo, nx), BF16)
+    stack_a[pl.ds(9 * cone, 16), :] = jnp.ones((16, cells + 2 * plane), BF16)
     for z in range(wide):
         for a in range(3):
             for b, y in ((0, 0), (2, ny - 1)):
@@ -111,40 +118,61 @@
     has_hi = de < nd - 1
     pl.semaphore_wait(bar, nsh - 1 + nz - 1)
 
-    def vol_copy(up):
-        src = vol.at[:, pl.ds(planes - 2, 2)] if up else vol.at[:, pl.ds(0, 2)]
-        side = 0 if up else 1
+    def vol_copy(side, i):
+        dist, at, count, start = parts[i]
+        src = planes - count if side == 0 else 0
+        dst = at if side == 0 else start
         return pltpu.make_async_remote_copy(
-            src_ref=src, dst_ref=vrecv.at[side], send_sem=vs_sem.at[side], recv_sem=vr_sem.at[side],
-            device_id=(dp, de + 1 if up else de - 1), device_id_type=MESH)
-
-    def slope_copy(up):
-        src = sl.at[planes - 1] if up else sl.at[0]
-        side = 0 if up else 1
+            src_ref=vol.at[:, pl.ds(src, count)], dst_ref=vrecv.at[side, :, pl.ds(dst, count)],
+            send_sem=vs_sem.at[side, i], recv_sem=vr_sem.at[side, i],
+            device_id=(dp, de + dist if side == 0 else de - dist), device_id_type=MESH)
+
+    def cot_copy(side):
         return pltpu.make_async_remote_copy(
-            src_ref=src, dst_ref=srecv.at[side], send_sem=ss_sem.at[side], recv_sem=sr_sem.at[side],
-            device_id=(dp, de + 1 if up else de - 1), device_id_type=MESH)
-
-    @pl.when(has_hi)
-    def _():
-        vol_copy(True).start()
-
-    @pl.when(has_lo)
-    def _():
-        vol_copy(False).start()
-
-    for side, has, z0 in ((0, has_lo, 0), (1, has_hi, planes + 2)):
-        @pl.when(has)
-        def _(side=side, z0=z0):
-            vol_copy(side == 0).wait_recv()
-            for ch in range(cin):
-                for z in range(2):
-                    v32[pl.ds((ch * wz + z0 + z) * ny, ny), :] = vrecv[side, ch, z].astype(F32)
-
-        @pl.when(jnp.logical_not(has))
-        def _(z0=z0):
-            for ch in range(cin):
-                for z in range(2):
+            src_ref=cot.at[:, pl.ds(planes - 1 if side == 0 else 0, 1)], dst_ref=crecv.at[side],
+            send_sem=ss_sem.at[side], recv_sem=sr_sem.at[side],
+            device_id=(dp, de + 1 if side == 0 else de - 1), device_id_type=MESH)
+
+    def sends(side, dist):
+        return de < nd - dist if side == 0 else de >= dist
+
+    def gets(side, dist):
+        return de >= dist if side == 0 else de < nd - dist
+
+    for i in range(len(parts)):
+        for side in range(2):
+            @pl.when(sends(side, parts[i][0]))
+            def _(side=side, i=i):
+                vol_copy(side, i).start()
+
+    for side in range(2):
+        @pl.when(sends(side, 1))
+        def _(side=side):
+            cot_copy(side).start()
+
+    for side in range(2):
+        z0 = 0 if side == 0 else planes + 3
+        filled = set()
+        for i, (dist, at, count, start) in enumerate(parts):
+            first = at if side == 0 else start
+            filled |= set(range(first, first + count))
+
+            @pl.when(gets(side, dist))
+            def _(side=side, i=i, first=first, count=count, z0=z0):
+                vol_copy(side, i).wait_recv()
+                for ch in range(cin):
+                    for z in range(first, first + count):
+                        v32[pl.ds((ch * wz + z0 + z) * ny, ny), :] = vrecv[side, ch, z].astype(F32)
+
+            @pl.when(jnp.logical_not(gets(side, dist)))
+            def _(first=first, count=count, z0=z0):
+                for ch in range(cin):
+                    for z in range(first, first + count):
+                        v32[pl.ds((ch * wz + z0 + z) * ny, ny), :] = zero8
+
+        for z in range(3):
+            if z not in filled:
+                for ch in range(cin):
                     v32[pl.ds((ch * wz + z0 + z) * ny, ny), :] = zero8
 
     row8 = lax.broadcasted_iota(jnp.int32, (8, nx), 0)
@@ -171,33 +199,39 @@
                    + left(res[pl.ds(2 * cone, cone), lanes], lane1) + bias1)
             s = 1.0 / (1.0 + jnp.exp(-pre))
             act = pre * s
-            if 1 <= zz <= planes:
-                d_one[:, pl.ds(((zz - 1) * ny + y) * nx, nx)] = s * (1.0 + pre * (1.0 - s))
-            elif zz == 0:
+            if 2 <= zz < planes + 2:
+                d_one[:, pl.ds(((zz - 2) * ny + y) * nx, nx)] = s * (1.0 + pre * (1.0 - s))
+            elif zz < 2:
                 act = jnp.where(has_lo, act, 0.0)
             else:
                 act = jnp.where(has_hi, act, 0.0)
             act = act.astype(BF16)
             for a in range(3):
                 z = zz - a
-                if not 0 <= z < planes:
+                if not 0 <= z < planes + 2:
                     continue
                 for b in range(3):
                     yo = y + 1 - b
                     if 0 <= yo < ny:
                         stack_a[pl.ds((a * 3 + b) * cone, cone), pl.ds((z * ny + yo) * nx, nx)] = act
 
+    def layer_two(z):
+        res[...] = jnp.dot(
+            lhs2, stack_a[pl.ds(0, 9 * cone), pl.ds((z + 1) * plane, plane)], preferred_element_type=F32)
+
+    def pre_two(y):
+        lanes = pl.ds(y * nx, nx)
+        return (right(res[pl.ds(0, ctwo), lanes], lane2) + res[pl.ds(ctwo, ctwo), lanes]
+                + left(res[pl.ds(2 * ctwo, ctwo), lanes], lane2) + bias2)
+
     for z in range(planes):
-        res[...] = jnp.dot(lhs2, stack_a[pl.ds(0, 9 * cone), pl.ds(z * plane, plane)], preferred_element_type=F32)
+        layer_two(z)
         for y in range(ny):
-            lanes = pl.ds(y * nx, nx)
-            pre = (right(res[pl.ds(0, ctwo), lanes], lane2) + res[pl.ds(ctwo, ctwo), lanes]
-                   + left(res[pl.ds(2 * ctwo, ctwo), lanes], lane2) + bias2)
+            pre = pre_two(y)
             s = 1.0 / (1.0 + jnp.exp(-pre))
             feat32[pl.ds(z * ny + y, ctwo, stride=planes * ny), :] = pre * s
             up = cot32[pl.ds(z * ny + y, ctwo, stride=planes * ny), :]
             slope = (up * (s * (1.0 + pre * (1.0 - s)))).astype(BF16)
-            sl[z, :, lanes] = slope
             slf = slope.astype(F32)
             cell = pl.ds((z * ny + y) * nx, nx)
             slope3[pl.ds(0, ctwo), cell] = left(slf, lane2).astype(BF16)
@@ -212,15 +246,7 @@
                     if 0 <= yo < ny:
                         stack_s[pl.ds((a * 3 + b) * ctwo, ctwo), pl.ds((zo * ny + yo) * nx, nx)] = slope
 
-    @pl.when(has_hi)
-    def _():
-        slope_copy(True).start()
-
-    @pl.when(has_lo)
-    def _():
-        slope_copy(False).start()
-
-    g2 = lax.dot_general(stack_a[...], slope3[...], NT, preferred_element_type=F32)
+    g2 = lax.dot_general(stack_a[:, pl.ds(plane, cells)], slope3[...], NT, preferred_element_type=F32)
     k2 = 9 * cone
     last = g2[0:k2, 2 * ctwo:3 * ctwo]
     tail = jnp.concatenate([last[0:k2 // 2], last[k2 // 2:k2]], axis=1).astype(BF16)
@@ -243,21 +269,28 @@
         def _():
             shard_copy(s).start()
 
-    for side, has, a, z in ((0, has_lo, 0, 0), (1, has_hi, 2, planes - 1)):
-        @pl.when(has)
-        def _(side=side):
-            slope_copy(side == 0).wait_recv()
-
-        @pl.when(jnp.logical_not(has))
-        def _(side=side):
-            srecv[side] = jnp.zeros((ctwo, plane), BF16)
-
-        for y in range(ny):
-            tile = srecv[side, :, pl.ds(y * nx, nx)]
+    for side, a, z in ((0, 0, 0), (1, 2, planes - 1)):
+        def place(y, tile, a=a, z=z):
             for b in range(3):
                 yo = y + 1 - b
                 if 0 <= yo < ny:
                     stack_s[pl.ds((a * 3 + b) * ctwo, ctwo), pl.ds((z * ny + yo) * nx, nx)] = tile
+
+        @pl.when(gets(side, 1))
+        def _(side=side, place=place):
+            layer_two(-1 if side == 0 else planes)
+            cot_copy(side).wait_recv()
+            ccot32[...] = crecv[side].astype(F32).reshape(ccot32.shape)
+            for y in range(ny):
+                pre = pre_two(y)
+                s = 1.0 / (1.0 + jnp.exp(-pre))
+                up = ccot32[pl.ds(y, ctwo, stride=ny), :]
+                place(y, (up * (s * (1.0 + pre * (1.0 - s)))).astype(BF16))
+
+        @pl.when(jnp.logical_not(gets(side, 1)))
+        def _(place=place):
+            for y in range(ny):
+                place(y, jnp.zeros((ctwo, nx), BF16))
 
     for z in range(planes):
         res[pl.ds(0, 3 * cone), :] = jnp.dot(
@@ -273,7 +306,7 @@
             slope31[pl.ds(cone, cone), cell] = slope
             slope31[pl.ds(2 * cone, cone), cell] = right(slf, lane1).astype(BF16)
 
-    g1 = lax.dot_general(stack_v[:, pl.ds(plane, cells)].astype(BF16), slope31[...], NT, preferred_element_type=F32)
+    g1 = lax.dot_general(stack_v[:, pl.ds(2 * plane, cells)].astype(BF16), slope31[...], NT, preferred_element_type=F32)
     g1 = jnp.concatenate([g1, jnp.zeros((72, nx - 3 * cone), F32)], axis=1)
     late = jnp.concatenate([g1, b2row], axis=0).astype(BF16)
     if cut < tail.shape[0]:
@@ -324,15 +357,15 @@
     drain(zb.at[pl.ds(0, nz - 1)], pzs)
     drain(gath.at[pl.ds(0, nsh - 1)], p2s)
 
-    @pl.when(has_hi)
-    def _():
-        vol_copy(True).wait_send()
-        slope_copy(True).wait_send()
-
-    @pl.when(has_lo)
-    def _():
-        vol_copy(False).wait_send()
-        slope_copy(False).wait_send()
+    for side in range(2):
+        for i in range(len(parts)):
+            @pl.when(sends(side, parts[i][0]))
+            def _(side=side, i=i):
+                vol_copy(side, i).wait_send()
+
+        @pl.when(sends(side, 1))
+        def _(side=side):
+            cot_copy(side).wait_send()
 
 
 def unpack(feat, packed, feat_o, g1_o, gb1_o, g2_o, gb2_o, g1, gb1, g2, gb2, sem):
@@ -391,16 +424,16 @@
             pltpu.VMEM((27, cone, ctwo), BF16),
             pltpu.VMEM((1, ctwo), F32),
             pltpu.VMEM((ctwo, planes, ny, nx), BF16),
-            pltpu.VMEM((2, cin, 2, ny, nx), BF16),
-            pltpu.VMEM((8 * (planes + 4) * ny, nx), F32),
-            pltpu.VMEM((72, (planes + 2) * ny * nx), F32),
+            pltpu.VMEM((2, cin, 3, ny, nx), BF16),
+            pltpu.VMEM((8 * (planes + 6) * ny, nx), F32),
+            pltpu.VMEM((72, (planes + 4) * ny * nx), F32),
             pltpu.VMEM((ctwo * planes * ny, nx), F32),
             pltpu.VMEM((cone, cells), F32),
-            pltpu.VMEM((9 * cone + 16, cells), BF16),
+            pltpu.VMEM((9 * cone + 16, cells + 2 * ny * nx), BF16),
             pltpu.VMEM((3 * ctwo, ny * nx), F32),
             pltpu.VMEM((3 * ctwo, cells), BF16),
-            pltpu.VMEM((planes, ctwo, ny * nx), BF16),
-            pltpu.VMEM((2, ctwo, ny * nx), BF16),
+            pltpu.VMEM((2, ctwo, 1, ny, nx), BF16),
+            pltpu.VMEM((ctwo * ny, nx), F32),
             pltpu.VMEM((9 * ctwo, cells), BF16),
             pltpu.VMEM((ctwo * planes * ny, nx), F32),
             pltpu.VMEM((3 * cone, cells), BF16),
@@ -410,7 +443,7 @@
             pltpu.VMEM((rows, nx), BF16),
             pltpu.VMEM((nsh, rows, nx), BF16),
             dma((6,)),
-            dma((2,)), dma((2,)), dma((2,)), dma((2,)),
+            dma((2, max(1, len(halo_parts(planes, nd))))), dma((2, max(1, len(halo_parts(planes, nd))))), dma((2,)), dma((2,)),
             dma, dma, dma, dma, dma, dma,
         ],
         compiler_params=pltpu.CompilerParams(

time: 27 us -> 23.4 us (0.87)
  Pallas kernels: 26.1 us -> 22.5 us
    pallas_call x1, Pallas kernels: 25.2 us -> 21.6 us  [per_device(): pl.pallas_call(functools.partial(kernel, ni, nz, nd), out_shape=(jax.Shap...]
where the time goes in v3:
time: 23.4 us; the launch traced here: 23.1 us
  Pallas kernels  22.5 us (96%)
  between operations  0.64 us (3%)
    pallas_call x1, Pallas kernels, per_device(): pl.pallas_call(functools.partial(kernel, ni, nz, nd), out_shape=(jax.Shap...  21.6 us
    pallas_call x1, Pallas kernels, per_device(): pl.pallas_call(unpack, out_shape=tuple((jax.ShapeDtypeStruct(*x) for x in...  0.92 us

profile of v3, /device:TPU:0, one launch (start us, length us, event | category | flops | bytes accessed | tf_op | source)
XLA Modules:
  0.0 23.1 jit_solution(10285744335153377895)
XLA Ops:
  0.6 21.6 %shard_map.101 = (bf16[64,2,8,128]{3,2,1,0:T(8,128)(2,1)S(1)}, bf16[512,128]{1,0:T(8,128)(2,1)S(1)}) custom-call(bf16[4,2,8,128]{3,2,1,0:T(8,128)(2,1)} %bitcast.22, bf16[27,4,32]{2,1,0:T(4,128)(2,1)} %bitcast.21, f32[1,32]{1,0:T(1,128)} %bitcast.23, bf16[27,32,64]{2,1,0:T(8,128)(2,1)} %bitcast.20, f32[1,64]{1,0:T(1,128)} %bitcast.24, ...), custom_call_target="tpu_custom_call" | custom-call | tf_op jit(solution)/shard_map/pallas_call | solution.py:412
  22.2 0.9 %shard_map.102 = (bf16[64,2,8,128]{3,2,1,0:T(8,128)(2,1)}, f32[27,4,32]{2,1,0:T(4,128)}, f32[1,32]{1,0:T(1,128)}, f32[27,32,64]{2,1,0:T(8,128)}, f32[1,64]{1,0:T(1,128)}) custom-call(bf16[64,2,8,128]{3,2,1,0:T(8,128)(2,1)S(1)} %get-tuple-element.12.feat, bf16[512,128]{1,0:T(8,128)(2,1)S(1)} %get-tuple-element.13.packed), custom_call_target="tpu_custom_call" | custom-call | tf_op jit(solution)/shard_map/pallas_call | solution.py:459

commit v4 on v3

--- a/solution.py
+++ b/solution.py
@@ -30,13 +30,29 @@
     plane = ny * nx
     wide = planes + 4
     parts = halo_parts(planes, nd)
-    nsh, rows = sb.shape[0], sb.shape[1]
+    halves, rows = zb.shape[0], sb.shape[1]
+    nsh = sb.shape[0] // halves
     early = (27 * cone * ctwo // nx) // rows
 
     de = lax.axis_index("depth")
     dp = lax.axis_index("dp")
     zi = lax.div(dp, ni)
     me = lax.rem(dp, ni) * nd + de
+
+    def peer(j):
+        return (zi * ni + lax.div(j, nd), lax.rem(j, nd))
+
+    def column(k):
+        return (k * ni + lax.rem(dp, ni), de)
+
+    bar = pltpu.get_barrier_semaphore()
+
+    for d in range(1, nz):
+        pl.semaphore_signal(bar, inc=1, device_id=column(lax.rem(zi + d, nz)), device_id_type=MESH)
+
+    @pl.loop(1, nsh)
+    def _(d):
+        pl.semaphore_signal(bar, inc=1, device_id=peer(lax.rem(me + d, nsh)), device_id_type=MESH)
 
     loads = [
         pltpu.make_async_copy(src, dst, in_sem.at[i])
@@ -45,21 +61,6 @@
     ]
     for copy in loads:
         copy.start()
-
-    def peer(j):
-        return (zi * ni + lax.div(j, nd), lax.rem(j, nd))
-
-    def column(k):
-        return (k * ni + lax.rem(dp, ni), de)
-
-    bar = pltpu.get_barrier_semaphore()
-
-    @pl.loop(1, nsh)
-    def _(d):
-        pl.semaphore_signal(bar, inc=1, device_id=peer(lax.rem(me + d, nsh)), device_id_type=MESH)
-
-    for d in range(1, nz):
-        pl.semaphore_signal(bar, inc=1, device_id=column(lax.rem(zi + d, nz)), device_id_type=MESH)
 
     wz = planes + 6
     zero8 = jnp.zeros((ny, nx), F32)
@@ -255,19 +256,20 @@
         [g2[0:k2, 0:2 * ctwo].astype(BF16), tail[0:cut]], axis=0).reshape(early, rows, nx)
     b2row = g2[k2:k2 + 8, 0:2 * ctwo]
 
-    def shard_copy(s):
+    def shard_copy(h, s):
         slot = lax.rem(me - s + nsh, nsh) - 1
         return pltpu.make_async_remote_copy(
-            src_ref=sb.at[s], dst_ref=rb.at[slot], send_sem=p1s, recv_sem=p1r,
+            src_ref=sb.at[h * nsh + s], dst_ref=rb.at[h, slot], send_sem=p1s, recv_sem=p1r.at[h],
             device_id=peer(s), device_id_type=MESH)
 
-    @pl.loop(1, nsh)
-    def _(d):
-        s = lax.rem(me + d, nsh)
-
-        @pl.when(s < early)
-        def _():
-            shard_copy(s).start()
+    for h in range(halves):
+        @pl.loop(1, nsh)
+        def _(d, h=h):
+            s = lax.rem(me + d, nsh)
+
+            @pl.when(h * nsh + s < early)
+            def _():
+                shard_copy(h, s).start()
 
     for side, a, z in ((0, 0, 0), (1, 2, planes - 1)):
         def place(y, tile, a=a, z=z):
@@ -311,51 +313,55 @@
     late = jnp.concatenate([g1, b2row], axis=0).astype(BF16)
     if cut < tail.shape[0]:
         late = jnp.concatenate([tail[cut:], late], axis=0)
-    sb[pl.ds(early, nsh - early)] = late.reshape(nsh - early, rows, nx)
-
-    @pl.loop(early, nsh)
-    def _(s):
-        @pl.when(s != me)
-        def _():
-            shard_copy(s).start()
+    sb[pl.ds(early, halves * nsh - early)] = late.reshape(halves * nsh - early, rows, nx)
+
+    for h in range(halves):
+        @pl.loop(max(early - h * nsh, 0), nsh)
+        def _(s, h=h):
+            @pl.when(s != me)
+            def _():
+                shard_copy(h, s).start()
 
     def drain(buf, sem):
         pltpu.make_async_copy(buf, buf, sem).wait()
 
-    drain(rb, p1r)
-    total = (sb[me].astype(F32) + jnp.sum(rb[...].astype(F32), axis=0)).astype(BF16)
-    zsrc[...] = total
-    zb[zi] = total
-
-    def z_copy(d):
+    def z_copy(h, d):
         return pltpu.make_async_remote_copy(
-            src_ref=zsrc, dst_ref=zb.at[zi], send_sem=pzs, recv_sem=pzr,
+            src_ref=zsrc.at[h], dst_ref=zb.at[h, zi], send_sem=pzs, recv_sem=pzr.at[h],
             device_id=column(lax.rem(zi + d, nz)), device_id_type=MESH)
 
-    for d in range(1, nz):
-        z_copy(d).start()
+    def out_copy(h, d):
+        return pltpu.make_async_remote_copy(
+            src_ref=gath.at[h * nsh + me], dst_ref=gath.at[h * nsh + me], send_sem=p2s, recv_sem=p2r,
+            device_id=peer(lax.rem(me + d, nsh)), device_id_type=MESH)
+
+    for h in range(halves):
+        drain(rb.at[h], p1r.at[h])
+        total = (sb[h * nsh + me].astype(F32) + jnp.sum(rb[h].astype(F32), axis=0)).astype(BF16)
+        zsrc[h] = total
+        zb[h, zi] = total
+        for d in range(1, nz):
+            z_copy(h, d).start()
+
     feat[...] = feat32[...].reshape(feat.shape).astype(BF16)
-    drain(zb.at[pl.ds(0, nz - 1)], pzr)
-    whole = zb[0].astype(F32)
-    for k in range(1, nz):
-        whole = whole + zb[k].astype(F32)
-    gath[me] = whole.astype(BF16)
-
-    def out_copy(d):
-        return pltpu.make_async_remote_copy(
-            src_ref=gath.at[me], dst_ref=gath.at[me], send_sem=p2s, recv_sem=p2r,
-            device_id=peer(lax.rem(me + d, nsh)), device_id_type=MESH)
-
-    @pl.loop(1, nsh)
-    def _(d):
-        out_copy(d).start()
-
-    drain(gath.at[pl.ds(0, nsh - 1)], p2r)
+    for h in range(halves):
+        drain(zb.at[h, pl.ds(0, nz - 1)], pzr.at[h])
+        whole = zb[h, 0].astype(F32)
+        for k in range(1, nz):
+            whole = whole + zb[h, k].astype(F32)
+        gath[h * nsh + me] = whole.astype(BF16)
+
+        @pl.loop(1, nsh)
+        def _(d, h=h):
+            out_copy(h, d).start()
+
+    others = pl.ds(0, halves * (nsh - 1))
+    drain(gath.at[others], p2r)
     packed[...] = gath[...].reshape(packed.shape)
 
-    drain(sb.at[pl.ds(0, nsh - 1)], p1s)
-    drain(zb.at[pl.ds(0, nz - 1)], pzs)
-    drain(gath.at[pl.ds(0, nsh - 1)], p2s)
+    drain(sb.at[others], p1s)
+    drain(gath.at[pl.ds(0, halves * (nz - 1))], pzs)
+    drain(gath.at[others], p2s)
 
     for side in range(2):
         for i in range(len(parts)):
@@ -403,7 +409,8 @@
     cells = planes * ny * nx
     total = 27 * cone * ctwo // nx + 80
     nsh = ni * nd
-    rows = total // nsh
+    halves = 2 if total // nsh % 32 == 0 else 1
+    rows = total // nsh // halves
     w1 = jnp.transpose(kernel_one, (2, 3, 4, 1, 0)).reshape(27, cin, cone)
     w2 = jnp.transpose(kernel_two, (2, 3, 4, 1, 0)).reshape(27, cone, ctwo)
     vm = pl.BlockSpec(memory_space=pltpu.VMEM)
@@ -437,14 +444,14 @@
             pltpu.VMEM((9 * ctwo, cells), BF16),
             pltpu.VMEM((ctwo * planes * ny, nx), F32),
             pltpu.VMEM((3 * cone, cells), BF16),
-            pltpu.VMEM((nsh, rows, nx), BF16),
-            pltpu.VMEM((nsh - 1, rows, nx), BF16),
-            pltpu.VMEM((nz, rows, nx), BF16),
-            pltpu.VMEM((rows, nx), BF16),
-            pltpu.VMEM((nsh, rows, nx), BF16),
+            pltpu.VMEM((halves * nsh, rows, nx), BF16),
+            pltpu.VMEM((halves, nsh - 1, rows, nx), BF16),
+            pltpu.VMEM((halves, nz, rows, nx), BF16),
+            pltpu.VMEM((halves, rows, nx), BF16),
+            pltpu.VMEM((halves * nsh, rows, nx), BF16),
             dma((6,)),
             dma((2, max(1, len(halo_parts(planes, nd))))), dma((2, max(1, len(halo_parts(planes, nd))))), dma((2,)), dma((2,)),
-            dma, dma, dma, dma, dma, dma,
+            dma, dma((halves,)), dma, dma((halves,)), dma, dma,
         ],
         compiler_params=pltpu.CompilerParams(
             collective_id=0, has_side_effects=True, vmem_limit_bytes=48 * 1024 * 1024),

time: 23.4 us -> 24.4 us (1.043)
  Pallas kernels: 22.5 us -> 23.5 us
    pallas_call x1, Pallas kernels: 21.6 us -> 22.5 us  [per_device(): pl.pallas_call(functools.partial(kernel, ni, nz, nd), out_shape=(jax.Shap...]
where the time goes in v4:
time: 24.4 us; the launch traced here: 24.1 us
  Pallas kernels  23.5 us (96%)
  between operations  0.64 us (3%)
    pallas_call x1, Pallas kernels, per_device(): pl.pallas_call(functools.partial(kernel, ni, nz, nd), out_shape=(jax.Shap...  22.5 us
    pallas_call x1, Pallas kernels, per_device(): pl.pallas_call(unpack, out_shape=tuple((jax.ShapeDtypeStruct(*x) for x in...  0.92 us

profile of v4, /device:TPU:0, one launch (start us, length us, event | category | flops | bytes accessed | tf_op | source)
XLA Modules:
  0.0 24.1 jit_solution(4704107996006111070)
XLA Ops:
  0.6 22.5 %shard_map.101 = (bf16[64,2,8,128]{3,2,1,0:T(8,128)(2,1)S(1)}, bf16[512,128]{1,0:T(8,128)(2,1)S(1)}) custom-call(bf16[4,2,8,128]{3,2,1,0:T(8,128)(2,1)} %bitcast.22, bf16[27,4,32]{2,1,0:T(4,128)(2,1)} %bitcast.21, f32[1,32]{1,0:T(1,128)} %bitcast.23, bf16[27,32,64]{2,1,0:T(8,128)(2,1)} %bitcast.20, f32[1,64]{1,0:T(1,128)} %bitcast.24, ...), custom_call_target="tpu_custom_call" | custom-call | tf_op jit(solution)/shard_map/pallas_call | solution.py:419
  23.2 0.9 %shard_map.102 = (bf16[64,2,8,128]{3,2,1,0:T(8,128)(2,1)}, f32[27,4,32]{2,1,0:T(4,128)}, f32[1,32]{1,0:T(1,128)}, f32[27,32,64]{2,1,0:T(8,128)}, f32[1,64]{1,0:T(1,128)}) custom-call(bf16[64,2,8,128]{3,2,1,0:T(8,128)(2,1)S(1)} %get-tuple-element.12.feat, bf16[512,128]{1,0:T(8,128)(2,1)S(1)} %get-tuple-element.13.packed), custom_call_target="tpu_custom_call" | custom-call | tf_op jit(solution)/shard_map/pallas_call | solution.py:466
